TPU v7x, 32 devices: a whole 2x2x4 slice. The times are simulated.
32 devices in a mesh: fsdp: 2 (over core), ctx: 4 (over z), tp: 4 (over y, x).
Axes of the slice: x: 2, y: 2, z: 4, core: 2. Of those that a mesh axis runs over, the one named last changes fastest.
Arguments:
- hidden_in: bfloat16 [8, 256, 1536], P('fsdp', 'ctx'), may hold values from -6 to 6
- segment_ids: int32 [8, 256], P('fsdp', 'ctx'), may hold values from 0 to 5, as said below
- doc_starts: int32 [8, 4], P('fsdp', 'ctx'), may hold values from 0 to 129, as said below
- norm1_gain: bfloat16 [1536], P(('fsdp', 'ctx')), may hold values from 0.5 to 1.5
- w_query: bfloat16 [1536, 1536], P(('fsdp', 'ctx'), 'tp'), may hold values from -0.15625 to 0.15625
- w_key: bfloat16 [1536, 1536], P(('fsdp', 'ctx'), 'tp'), may hold values from -0.15625 to 0.15625
- w_value: bfloat16 [1536, 1536], P(('fsdp', 'ctx'), 'tp'), may hold values from -0.15625 to 0.15625
- w_house: bfloat16 [1536, 1536], P(('fsdp', 'ctx'), 'tp'), may hold values from -0.15625 to 0.15625
- w_beta: bfloat16 [1536, 12], P(('fsdp', 'ctx'), 'tp'), may hold values from -0.5 to 0.5
- w_out: bfloat16 [1536, 1536], P(('fsdp', 'ctx'), 'tp'), may hold values from -0.625 to 0.625
- norm2_gain: bfloat16 [1536], P(('fsdp', 'ctx')), may hold values from 0.5 to 1.5
- w_gate: bfloat16 [1536, 4096], P(('fsdp', 'ctx'), 'tp'), may hold values from -0.15625 to 0.15625
- w_up: bfloat16 [1536, 4096], P(('fsdp', 'ctx'), 'tp'), may hold values from -0.15625 to 0.15625
- w_down: bfloat16 [1536, 4096], P(('fsdp', 'ctx'), 'tp'), may hold values from -0.09375 to 0.09375
- output_grad: bfloat16 [8, 256, 1536], P('fsdp', 'ctx'), may hold values from -6 to 6
Outputs:
- block_out: bfloat16 [8, 256, 1536], P('fsdp', 'ctx')
- input_grad: bfloat16 [8, 256, 1536], P('fsdp', 'ctx')
- norm1_gain_grad: float32 [1536], P(('fsdp', 'ctx'))
- w_query_grad: float32 [1536, 1536], P(('fsdp', 'ctx'), 'tp')
- w_key_grad: float32 [1536, 1536], P(('fsdp', 'ctx'), 'tp')
- w_value_grad: float32 [1536, 1536], P(('fsdp', 'ctx'), 'tp')
- w_house_grad: float32 [1536, 1536], P(('fsdp', 'ctx'), 'tp')
- w_beta_grad: float32 [1536, 12], P(('fsdp', 'ctx'), 'tp')
- w_out_grad: float32 [1536, 1536], P(('fsdp', 'ctx'), 'tp')
- norm2_gain_grad: float32 [1536], P(('fsdp', 'ctx'))
- w_gate_grad: float32 [1536, 4096], P(('fsdp', 'ctx'), 'tp')
- w_up_grad: float32 [1536, 4096], P(('fsdp', 'ctx'), 'tp')
- w_down_grad: float32 [1536, 4096], P(('fsdp', 'ctx'), 'tp')
Inputs may be any that keep to these rules, and one draw needn't show every extreme that they name: `segment_ids`: ids never fall along a sequence; each sequence holds 6 documents, numbered in order from 0; the last document of each sequence begins one position after the first position of its second-to-last group and runs to the end. `doc_starts`: for group c of 64 positions, the position within the sequence where the document that holds position c * 64 begins, as given by segment_ids; it is at most c * 64.
All inputs are finite; a program needn't handle non-finite values.
Results may differ from a plain program's by a relative error of at most 0.02.
Values may be sent and summed in bfloat16 or wider, within the bound.
No kernel may reach another device: no remote copies, remote signals or barrier semaphores. Data moves between devices by JAX's collectives and lax.ppermute only.
A program may use at most 128 MiB of HBM per device.

v0:
```python
import math

import jax
import jax.numpy as jnp
from jax import lax
from jax.sharding import PartitionSpec as P

EPSILON = 1e-06
HIGHEST = lax.Precision.HIGHEST
NEGATIVE = -1e30


def passed_along(block, axis, distance):
    devices = range(lax.axis_size(axis))
    route = [(i - distance, i) for i in devices if i - distance in devices]
    return lax.ppermute(block, axis, route)


def group_algebra(queries, key_rows, house, betas):
    length = queries.shape[0]
    scaling = 1.0 / math.sqrt(queries.shape[1])
    row_index = lax.broadcasted_iota(jnp.int32, (length, length), 0)
    column_index = lax.broadcasted_iota(jnp.int32, (length, length), 1)
    strict_below = row_index > column_index
    house_gram = jnp.dot(house, house.T, precision=HIGHEST)
    system = jnp.where(strict_below, house_gram, 0.0) + jnp.diag(1.0 / betas)
    identity = jnp.eye(length, dtype=house.dtype)
    inverse = jax.scipy.linalg.solve_triangular(system, identity, lower=True)
    query_house = jnp.where(
        row_index >= column_index, jnp.dot(queries, house.T, precision=HIGHEST), 0.0
    )
    house_key = jnp.where(strict_below, jnp.dot(house, key_rows.T, precision=HIGHEST), 0.0)
    query_side = jnp.dot(query_house, inverse, precision=HIGHEST)
    key_side = jnp.dot(inverse, house_key, precision=HIGHEST)
    scores = (
        jnp.dot(queries, key_rows.T, precision=HIGHEST)
        - jnp.dot(query_side, house_key, precision=HIGHEST)
    ) * scaling
    query_bar = queries - jnp.dot(query_side, house, precision=HIGHEST)
    key_bar = key_rows - jnp.dot(key_side.T, house, precision=HIGHEST)
    inner = jnp.dot(inverse, house, precision=HIGHEST)
    factor = jnp.eye(house.shape[1], dtype=house.dtype) - jnp.dot(house.T, inner, precision=HIGHEST)
    return (scores, query_bar, key_bar, factor)


def local_map(queries, key_rows, house_raw, beta_logits):
    house = house_raw * lax.rsqrt(jnp.sum(house_raw * house_raw, axis=-1, keepdims=True) + EPSILON)
    betas = 2.0 * jax.nn.sigmoid(beta_logits)
    return jax.vmap(jax.vmap(group_algebra))(queries, key_rows, house, betas)


def doc_starts_local(segment_ids, group_first, first_position):
    offsets = lax.broadcasted_iota(jnp.int32, segment_ids.shape, segment_ids.ndim - 1)
    previous = jnp.concatenate([segment_ids[..., :1], segment_ids[..., :-1]], axis=-1)
    boundary = (offsets > 0) & (segment_ids != previous)
    marks = jnp.where(boundary, offsets + first_position, -1)
    return jnp.maximum(lax.cummax(marks, axis=segment_ids.ndim - 1), group_first)


def norm_rows(values):
    factor = lax.rsqrt(jnp.mean(values * values, axis=-1, keepdims=True) + EPSILON)
    return (values * factor, factor)


def norm_back(gradient, normed, factor, norm_gain):
    scaled = gradient * norm_gain
    return factor * (scaled - normed * jnp.mean(scaled * normed, axis=-1, keepdims=True))


def split_heads(tensor, head_count):
    seq_count, length, total_width = tensor.shape
    return tensor.reshape(seq_count, length, head_count, total_width // head_count).transpose(
        0, 2, 1, 3
    )


def join_heads(tensor):
    seq_count, head_count, length, head_width = tensor.shape
    return tensor.transpose(0, 2, 1, 3).reshape(seq_count, length, head_count * head_width)


def project(inputs, weight):
    return jnp.einsum("scd,df->scf", inputs, weight, preferred_element_type=jnp.float32)


def project_back(gradient, weight):
    return jnp.einsum("scf,df->scd", gradient, weight, preferred_element_type=jnp.float32)


def weight_grad(inputs, gradient):
    return jnp.einsum("scd,scf->df", inputs, gradient, preferred_element_type=jnp.float32)


def cross_scores(query_rot, key_low, scaling):
    return (
        jnp.einsum("shqd,shkd->shqk", query_rot, key_low, preferred_element_type=jnp.float32)
        * scaling
    )


def weighted_values(weights, values_in):
    return jnp.einsum("shqk,shkd->shqd", weights, values_in, preferred_element_type=jnp.float32)


def shards(
    hidden_in,
    segment_ids,
    doc_starts,
    norm1_gain,
    w_query,
    w_key,
    w_value,
    w_house,
    w_beta,
    w_out,
    norm2_gain,
    w_gate,
    w_up,
    w_down,
    output_grad,
):
    gathered = (
        lax.all_gather(norm1_gain, ("fsdp", "ctx"), axis=0, tiled=True),
        lax.all_gather(w_query, ("fsdp", "ctx"), axis=0, tiled=True),
        lax.all_gather(w_key, ("fsdp", "ctx"), axis=0, tiled=True),
        lax.all_gather(w_value, ("fsdp", "ctx"), axis=0, tiled=True),
        lax.all_gather(w_house, ("fsdp", "ctx"), axis=0, tiled=True),
        lax.all_gather(w_beta, ("fsdp", "ctx"), axis=0, tiled=True),
        lax.all_gather(w_out, ("fsdp", "ctx"), axis=0, tiled=True),
        lax.all_gather(norm2_gain, ("fsdp", "ctx"), axis=0, tiled=True),
        lax.all_gather(w_gate, ("fsdp", "ctx"), axis=0, tiled=True),
        lax.all_gather(w_up, ("fsdp", "ctx"), axis=0, tiled=True),
        lax.all_gather(w_down, ("fsdp", "ctx"), axis=0, tiled=True),
    )
    (
        gain_one,
        query_full,
        key_full,
        value_full,
        house_full,
        beta_full,
        out_full,
        gain_two,
        gate_full,
        up_full,
        down_full,
    ) = gathered
    gain_one_f = gain_one.astype(jnp.float32)
    gain_two_f = gain_two.astype(jnp.float32)
    head_count = beta_full.shape[1]
    length = hidden_in.shape[1]
    residual = hidden_in.astype(jnp.float32)
    normed_one, factor_one = norm_rows(residual)
    h_one = (normed_one * gain_one_f).astype(jnp.bfloat16)
    queries = split_heads(project(h_one, query_full), head_count)
    key_rows = split_heads(project(h_one, key_full), head_count)
    values_low = split_heads(project(h_one, value_full).astype(jnp.bfloat16), head_count)
    house_raw = split_heads(project(h_one, house_full), head_count)
    beta_logits = project(h_one, beta_full).transpose(0, 2, 1)
    (scores_local, query_bar, key_bar, factors), local_back = jax.vjp(
        local_map, queries, key_rows, house_raw, beta_logits
    )
    scaling = 1.0 / math.sqrt(queries.shape[-1])
    chain_index = lax.axis_index("ctx")
    hop_total = lax.axis_size("ctx") - 1
    first_position = chain_index * length
    starts = doc_starts_local(segment_ids, doc_starts, first_position)
    offsets = jnp.arange(length, dtype=jnp.int32)
    causal = (offsets[None, :] <= offsets[:, None])[None]
    local_mask = (causal & (offsets[None, None, :] + first_position >= starts[:, :, None]))[:, None]

    def hop_mask(distance):
        key_pos = (chain_index - distance) * length + offsets
        return (key_pos[None, None, :] >= starts[:, :, None])[:, None]

    masked_local = jnp.where(local_mask, scores_local, NEGATIVE)
    local_max = jnp.max(masked_local, axis=-1)
    local_sum = jnp.sum(jnp.exp(masked_local - local_max[..., None]), axis=-1)
    key_send = key_bar.astype(jnp.bfloat16)
    identity = jnp.broadcast_to(jnp.eye(factors.shape[-1], dtype=jnp.float32), factors.shape)
    stack_rot = jnp.zeros((hop_total,) + query_bar.shape, jnp.bfloat16)
    stack_factors = jnp.zeros((hop_total,) + factors.shape, jnp.float32)

    def rotate(hop_step, hop_keys, chain, run_max, run_sum):
        query_rot = jnp.einsum("shqa,shab->shqb", query_bar, chain, precision=HIGHEST).astype(
            jnp.bfloat16
        )
        masked = jnp.where(
            hop_mask(hop_step + 1), cross_scores(query_rot, hop_keys, scaling), NEGATIVE
        )
        new_max = jnp.maximum(run_max, jnp.max(masked, axis=-1))
        new_sum = run_sum * jnp.exp(run_max - new_max) + jnp.sum(
            jnp.exp(masked - new_max[..., None]), axis=-1
        )
        return (query_rot, new_max, new_sum)

    stack_keys = jnp.zeros((hop_total,) + key_send.shape, jnp.bfloat16)
    stack_values = jnp.zeros((hop_total,) + values_low.shape, jnp.bfloat16)

    def forward_hop(hop_step, loop_state):
        (
            send_keys,
            send_values,
            send_factor,
            kept_keys,
            kept_values,
            kept_rot,
            kept_factors,
            run_max,
            run_sum,
        ) = loop_state
        got_keys, got_values = passed_along((send_keys, send_values), "ctx", 1)
        got_factor = passed_along(send_factor.astype(jnp.bfloat16), "ctx", 1).astype(
            send_factor.dtype
        )
        query_rot, run_max, run_sum = rotate(hop_step, got_keys, got_factor, run_max, run_sum)
        kept_keys = lax.dynamic_update_index_in_dim(kept_keys, got_keys, hop_step, 0)
        kept_values = lax.dynamic_update_index_in_dim(kept_values, got_values, hop_step, 0)
        kept_rot = lax.dynamic_update_index_in_dim(kept_rot, query_rot, hop_step, 0)
        kept_factors = lax.dynamic_update_index_in_dim(kept_factors, got_factor, hop_step, 0)
        next_factor = jnp.einsum("shab,shbc->shac", factors, got_factor, precision=HIGHEST)
        return (
            got_keys,
            got_values,
            next_factor,
            kept_keys,
            kept_values,
            kept_rot,
            kept_factors,
            run_max,
            run_sum,
        )

    loop_state = lax.fori_loop(
        0,
        hop_total,
        forward_hop,
        (
            key_send,
            values_low,
            identity,
            stack_keys,
            stack_values,
            stack_rot,
            stack_factors,
            local_max,
            local_sum,
        ),
    )
    stack_keys, stack_values, stack_rot, stack_factors = (
        loop_state[3],
        loop_state[4],
        loop_state[5],
        loop_state[6],
    )
    run_max, run_sum = (loop_state[7], loop_state[8])

    def fetch(hop_step):
        return (
            lax.dynamic_index_in_dim(stack_keys, hop_step, 0, keepdims=False),
            lax.dynamic_index_in_dim(stack_values, hop_step, 0, keepdims=False),
        )

    log_total = run_max + jnp.log(run_sum)

    def recall(hop_step):
        hop_keys, hop_values = fetch(hop_step)
        hop_factor = lax.dynamic_index_in_dim(stack_factors, hop_step, 0, keepdims=False)
        query_rot = lax.dynamic_index_in_dim(stack_rot, hop_step, 0, keepdims=False)
        masked = jnp.where(
            hop_mask(hop_step + 1), cross_scores(query_rot, hop_keys, scaling), NEGATIVE
        )
        hop_probs = jnp.exp(masked - log_total[..., None])
        return (hop_keys, hop_values, hop_factor, query_rot, hop_probs)

    probs_local = jnp.exp(masked_local - log_total[..., None])
    probs_local_low = probs_local.astype(jnp.bfloat16)
    attn_acc = weighted_values(probs_local_low, values_low)
    attn_rest = weighted_values(
        (probs_local - probs_local_low.astype(jnp.float32)).astype(jnp.bfloat16), values_low
    )

    def value_hop(hop_step, running):
        total_low, total_rest = running
        hop_keys, hop_values, hop_factor, query_rot, hop_probs = recall(hop_step)
        hop_low = hop_probs.astype(jnp.bfloat16)
        total_low = total_low + weighted_values(hop_low, hop_values)
        total_rest = total_rest + weighted_values(
            (hop_probs - hop_low.astype(jnp.float32)).astype(jnp.bfloat16), hop_values
        )
        return (total_low, total_rest)

    attn_acc, attn_rest = lax.fori_loop(0, hop_total, value_hop, (attn_acc, attn_rest))
    attn_low = join_heads(attn_acc.astype(jnp.bfloat16))
    branch = lax.psum(project_back(attn_low, out_full), "tp")
    middle = residual + branch
    normed_two, factor_two = norm_rows(middle)
    h_two = (normed_two * gain_two_f).astype(jnp.bfloat16)
    gate_proj = project(h_two, gate_full)
    up_proj = project(h_two, up_full)
    gate_sigmoid = jax.nn.sigmoid(gate_proj)
    silu_gate = gate_proj * gate_sigmoid
    hidden_low = (silu_gate * up_proj).astype(jnp.bfloat16)
    mlp_out = lax.psum(project_back(hidden_low, down_full).astype(jnp.bfloat16), "tp").astype(
        jnp.float32
    )
    block_out = (middle + mlp_out).astype(jnp.bfloat16)
    down_grad = weight_grad(output_grad, hidden_low)
    d_hidden = project(output_grad, down_full)
    d_gate = (d_hidden * up_proj * gate_sigmoid * (1.0 + gate_proj * (1.0 - gate_sigmoid))).astype(
        jnp.bfloat16
    )
    d_up = (d_hidden * silu_gate).astype(jnp.bfloat16)
    gate_grad = weight_grad(h_two, d_gate)
    up_grad = weight_grad(h_two, d_up)
    d_two = lax.psum(project_back(d_gate, gate_full) + project_back(d_up, up_full), "tp")
    gain_two_grad = jnp.sum(d_two * normed_two, axis=(0, 1))
    d_middle = output_grad.astype(jnp.float32) + norm_back(
        d_two, normed_two, factor_two, gain_two_f
    )
    d_branch = d_middle.astype(jnp.bfloat16)
    out_grad = weight_grad(d_branch, attn_low)
    d_attn = split_heads(project(d_branch, out_full).astype(jnp.bfloat16), head_count)
    d_probs_local = jnp.einsum(
        "shqd,shkd->shqk", d_attn, values_low, preferred_element_type=jnp.float32
    )
    row_delta = jnp.sum(d_attn.astype(jnp.float32) * (attn_acc + attn_rest), axis=-1)
    zero_factor = jnp.zeros(factors.shape, jnp.float32)
    zero_bar = jnp.zeros(query_bar.shape, jnp.float32)

    def back_hop(back_step, loop_state):
        carry_keys, carry_values, carry_factor, d_bar, d_factors = loop_state
        hop_step = hop_total - 1 - back_step
        hop_keys, hop_values, hop_factor, query_rot, hop_probs = recall(hop_step)
        d_probs = jnp.einsum(
            "shqd,shkd->shqk", d_attn, hop_values, preferred_element_type=jnp.float32
        )
        d_cross = (hop_probs * (d_probs - row_delta[..., None])).astype(jnp.bfloat16)
        d_rot = (
            jnp.einsum("shqk,shkd->shqd", d_cross, hop_keys, preferred_element_type=jnp.float32)
            * scaling
        )
        d_bar = d_bar + jnp.einsum("shqb,shab->shqa", d_rot, hop_factor, precision=HIGHEST)
        factor_local = jnp.einsum("shqa,shqb->shab", query_bar, d_rot, precision=HIGHEST)
        keys_total = (
            carry_keys
            + jnp.einsum("shqk,shqd->shkd", d_cross, query_rot, preferred_element_type=jnp.float32)
            * scaling
        )
        values_total = carry_values + jnp.einsum(
            "shqk,shqd->shkd",
            hop_probs.astype(jnp.bfloat16),
            d_attn,
            preferred_element_type=jnp.float32,
        )
        factor_total = factor_local + jnp.einsum(
            "shba,shbc->shac", factors, carry_factor, precision=HIGHEST
        )
        d_factors = d_factors + jnp.einsum(
            "shac,shbc->shab", carry_factor, hop_factor, precision=HIGHEST
        )
        carry_keys, carry_values, carry_factor = (
            passed_along(keys_total.astype(jnp.bfloat16), "ctx", -1).astype(keys_total.dtype),
            passed_along(values_total.astype(jnp.bfloat16), "ctx", -1).astype(values_total.dtype),
            passed_along(factor_total.astype(jnp.bfloat16), "ctx", -1).astype(factor_total.dtype),
        )
        return (carry_keys, carry_values, carry_factor, d_bar, d_factors)

    zero_rows = jnp.zeros(key_send.shape, jnp.float32)
    loop_state = lax.fori_loop(
        0, hop_total, back_hop, (zero_rows, zero_rows, zero_factor, zero_bar, zero_factor)
    )
    carry_keys, carry_values, d_bar, d_factors = (
        loop_state[0],
        loop_state[1],
        loop_state[3],
        loop_state[4],
    )
    d_local = probs_local * (d_probs_local - row_delta[..., None])
    values_sum = carry_values + jnp.einsum(
        "shqk,shqd->shkd", probs_local_low, d_attn, preferred_element_type=jnp.float32
    )
    d_queries, d_keys, d_house, d_betas = local_back((d_local, d_bar, carry_keys, d_factors))
    query_low = join_heads(d_queries.astype(jnp.bfloat16))
    key_low = join_heads(d_keys.astype(jnp.bfloat16))
    value_low = join_heads(values_sum.astype(jnp.bfloat16))
    house_low = join_heads(d_house.astype(jnp.bfloat16))
    beta_low = d_betas.transpose(0, 2, 1).astype(jnp.bfloat16)
    query_grad = weight_grad(h_one, query_low)
    key_grad = weight_grad(h_one, key_low)
    value_grad = weight_grad(h_one, value_low)
    house_grad = weight_grad(h_one, house_low)
    beta_grad = weight_grad(h_one, beta_low)
    partial_one = (
        project_back(query_low, query_full)
        + project_back(key_low, key_full)
        + project_back(value_low, value_full)
    )
    partial_one = (
        partial_one + project_back(house_low, house_full) + project_back(beta_low, beta_full)
    )
    d_one = lax.psum(partial_one.astype(jnp.bfloat16), "tp").astype(jnp.float32)
    gain_one_grad = jnp.sum(d_one * normed_one, axis=(0, 1))
    input_grad = (d_middle + norm_back(d_one, normed_one, factor_one, gain_one_f)).astype(
        jnp.bfloat16
    )
    results = tuple(
        (
            lax.psum_scatter(
                gain_one_grad.astype(jnp.bfloat16), ("fsdp", "ctx"), scatter_dimension=0, tiled=True
            ).astype(jnp.float32),
            lax.psum_scatter(
                query_grad.astype(jnp.bfloat16), ("fsdp", "ctx"), scatter_dimension=0, tiled=True
            ).astype(jnp.float32),
            lax.psum_scatter(
                key_grad.astype(jnp.bfloat16), ("fsdp", "ctx"), scatter_dimension=0, tiled=True
            ).astype(jnp.float32),
            lax.psum_scatter(
                value_grad.astype(jnp.bfloat16), ("fsdp", "ctx"), scatter_dimension=0, tiled=True
            ).astype(jnp.float32),
            lax.psum_scatter(
                house_grad.astype(jnp.bfloat16), ("fsdp", "ctx"), scatter_dimension=0, tiled=True
            ).astype(jnp.float32),
            lax.psum_scatter(
                beta_grad.astype(jnp.bfloat16), ("fsdp", "ctx"), scatter_dimension=0, tiled=True
            ).astype(jnp.float32),
            lax.psum_scatter(
                out_grad.astype(jnp.bfloat16), ("fsdp", "ctx"), scatter_dimension=0, tiled=True
            ).astype(jnp.float32),
            lax.psum_scatter(
                gain_two_grad.astype(jnp.bfloat16), ("fsdp", "ctx"), scatter_dimension=0, tiled=True
            ).astype(jnp.float32),
            lax.psum_scatter(
                gate_grad.astype(jnp.bfloat16), ("fsdp", "ctx"), scatter_dimension=0, tiled=True
            ).astype(jnp.float32),
            lax.psum_scatter(
                up_grad.astype(jnp.bfloat16), ("fsdp", "ctx"), scatter_dimension=0, tiled=True
            ).astype(jnp.float32),
            lax.psum_scatter(
                down_grad.astype(jnp.bfloat16), ("fsdp", "ctx"), scatter_dimension=0, tiled=True
            ).astype(jnp.float32),
        )
    )
    return (block_out, input_grad) + results


def solution(mesh):
    in_specs = (
        P("fsdp", "ctx", None),
        P("fsdp", "ctx"),
        P("fsdp", "ctx"),
        P(("fsdp", "ctx")),
        P(("fsdp", "ctx"), "tp"),
        P(("fsdp", "ctx"), "tp"),
        P(("fsdp", "ctx"), "tp"),
        P(("fsdp", "ctx"), "tp"),
        P(("fsdp", "ctx"), "tp"),
        P(("fsdp", "ctx"), "tp"),
        P(("fsdp", "ctx")),
        P(("fsdp", "ctx"), "tp"),
        P(("fsdp", "ctx"), "tp"),
        P(("fsdp", "ctx"), "tp"),
        P("fsdp", "ctx", None),
    )
    out_specs = (
        P("fsdp", "ctx", None),
        P("fsdp", "ctx", None),
        P(("fsdp", "ctx")),
        P(("fsdp", "ctx"), "tp"),
        P(("fsdp", "ctx"), "tp"),
        P(("fsdp", "ctx"), "tp"),
        P(("fsdp", "ctx"), "tp"),
        P(("fsdp", "ctx"), "tp"),
        P(("fsdp", "ctx"), "tp"),
        P(("fsdp", "ctx")),
        P(("fsdp", "ctx"), "tp"),
        P(("fsdp", "ctx"), "tp"),
        P(("fsdp", "ctx"), "tp"),
    )
    return jax.shard_map(shards, mesh=mesh, in_specs=in_specs, out_specs=out_specs, check_vma=False)
```

profile of v0, /device:TPU:0, one launch (start us, length us, event | category | flops | bytes accessed | tf_op | source)
XLA Modules:
  0.0 1143.7 jit_solution(5119565101753351843)
XLA Ops:
  15.1 20.2 %all-reduce.5 = (bf16[1536]{0:T(1024)(128)(2,1)S(1)}, bf16[1536]{0:T(1024)(128)(2,1)}) all-reduce(bf16[1536]{0:T(1024)(128)(2,1)S(1)} %dynamic-update-slice, bf16[1536]{0:T(1024)(128)(2,1)S(1)} %dynamic-update-slice.1), channel_id=1, replica_groups=mesh['fsdp'=2,'ctx'=4,'tp'=4] {'fsdp','ctx'}, use_global_device_ids=true, to_apply=%add | all-reduce | flops 3072 | bytes 12288
  36.7 21.9 %all-gather = bf16[8,192,3]{1,2,0:T(4,128)(2,1)S(1)} all-gather(bf16[1,192,3]{1,2,0:T(4,128)(2,1)S(1)} %bitcast.471), channel_id=1, replica_groups=mesh['fsdp'=2,'ctx'=4,'tp'=4] {'fsdp','ctx'}, dimensions={0}, use_global_device_ids=true | all-gather | bytes 10368 | tf_op jit(solution)/shard_map/all_gather | solution.py:128
  66.5 17.4 %all-gather.10.cloned.1.call-done = bf16[1536,384]{1,0:T(8,128)(2,1)} async-done(((bf16[192,384]{1,0:T(8,128)(2,1)}), bf16[1536,384]{1,0:T(8,128)(2,1)}) %all-gather.10.cloned.1.call-update) | async-done | bytes 1179664 | tf_op jit(solution)/shard_map/all_gather | solution.py:124
  91.4 59.9 %custom-call.7 = f32[4,3,1,64,64]{3,4,2,1,0:T(8,128)S(1)} custom-call(f32[4,3,1,64,64]{4,3,2,1,0:T(8,128)} %fusion.117), custom_call_target="InvertDiagBlocksLowerTriangular" | custom-call | tf_op jit(solution)/shard_map/jvp(vmap(vmap(jit(_solve_triangular))))/triangular_solve | solution.py:28
  164.6 77.4 %while.70 = (s32[]{:T(128)}, bf16[4,3,64,128]{3,2,1,0:T(8,128)(2,1)}, bf16[4,3,64,128]{3,2,1,0:T(8,128)(2,1)}, bf16[4,3,128,128]{3,2,1,0:T(8,128)(2,1)}, bf16[3,...) while((s32[]{:T(128)}, ...), condition=%wide.region_8.9_spmd.clone, body=%wide.region_5.8_spmd.clone.sunk | while | flops 466126400 | bytes 9536377 | solution.py:234
  164.6 3.4 collective-permute-start.2
  168.0 3.1 collective-permute-start
  171.0 2.6 collective-permute-start.1
  174.5 7.5 collective-permute-done
  182.6 2.9 collective-permute-done.1
  190.6 4.3 collective-permute-start.2
  194.9 3.1 collective-permute-start
  198.0 2.6 collective-permute-start.1
  201.4 7.6 collective-permute-done
  216.8 4.3 collective-permute-start.2
  221.1 3.1 collective-permute-start
  224.1 2.6 collective-permute-start.1
  227.5 7.2 collective-permute-done
  245.6 7.6 while.71
  253.3 3.5 fusion.120
  259.6 58.9 %all-reduce.11.cloned.1.call-done = f32[4,64,1536]{2,1,0:T(8,128)} async-done(((f32[4,64,1536]{2,1,0:T(8,128)}), f32[4,64,1536]{2,1,0:T(8,128)}) %all-reduce.11.cloned.1.call-update) | async-done | bytes 1572880 | tf_op jit(solution)/shard_map/psum | solution.py:295
  321.9 36.6 %all-gather.22.cloned.1.call-done = bf16[1536,1024]{1,0:T(8,128)(2,1)} async-done(((bf16[192,1024]{1,0:T(8,128)(2,1)}), bf16[1536,1024]{1,0:T(8,128)(2,1)}) %all-gather.22.cloned.1.call-update) | async-done | bytes 3145744 | tf_op jit(solution)/shard_map/all_gather | solution.py:132
  358.5 4.1 fusion.72
  362.6 34.8 %all-gather.24.cloned.1.call-done = bf16[1536,1024]{1,0:T(8,128)(2,1)} async-done(((bf16[192,1024]{1,0:T(8,128)(2,1)}), bf16[1536,1024]{1,0:T(8,128)(2,1)}) %all-gather.24.cloned.1.call-update) | async-done | bytes 3145744 | tf_op jit(solution)/shard_map/all_gather | solution.py:133
  397.4 3.8 fusion.66
  401.2 35.0 %all-gather.20.cloned.1.call-done = bf16[1536,1024]{1,0:T(8,128)(2,1)} async-done(((bf16[192,1024]{1,0:T(8,128)(2,1)}), bf16[1536,1024]{1,0:T(8,128)(2,1)}) %all-gather.20.cloned.1.call-update) | async-done | bytes 3145744 | tf_op jit(solution)/shard_map/all_gather | solution.py:131
  436.3 5.1 multiply_convert_fusion.2
  446.0 2.3 copy.195
  448.2 4.0 fusion.87
  452.3 53.5 %all-reduce.13.cloned.1.call-done = f32[4,64,1536]{2,1,0:T(8,128)} async-done(((f32[4,64,1536]{2,1,0:T(8,128)}), f32[4,64,1536]{2,1,0:T(8,128)}) %all-reduce.13.cloned.1.call-update) | async-done | bytes 1572880 | tf_op jit(solution)/shard_map/psum | solution.py:316
  505.8 2.6 multiply_reduce_fusion
  513.2 96.0 %while.72 = (s32[]{:T(128)}, f32[4,3,64,128]{3,2,1,0:T(8,128)}, f32[4,3,64,128]{3,2,1,0:T(8,128)}, f32[4,3,128,128]{2,3,1,0:T(8,128)S(1)}, f32[4,3,64,128]{3,2,1...) while((s32[]{:T(128)}, f32[4,3,64,128]{3,2,1,0:T(8,128)}, ...), condition=%wide.region_18.19_spmd.clone, body=%wide.region_17.18_spmd.clone.sunk | while | flops 971800640 | bytes 25902632 | solution.py:370
  519.6 2.2 fusion.412
  528.5 2.9 fusion.413
  531.4 3.5 convolution_add_fusion.23
  534.9 5.3 collective-permute-done.3
  552.4 2.2 fusion.412
  561.3 3.2 fusion.413
  564.5 3.6 convolution_add_fusion.23
  568.1 5.0 collective-permute-done.3
  593.3 3.2 fusion.413
  596.5 3.6 convolution_add_fusion.23
  600.1 4.1 collective-permute-done.3
  609.3 2.8 fusion.153
  628.0 2.3 fusion.161
  645.6 3.0 fusion.84
  650.4 2.9 fusion.83
  653.4 2.9 fusion.82
  656.7 2.9 fusion.81
  659.7 4.0 fusion.65
  663.6 4.6 copy.255
  668.4 4.0 bitcast_convert_fusion.2
  672.4 4.0 bitcast_convert_fusion.1
  678.7 54.9 %all-reduce.15.cloned.1.call-done = (bf16[4,64,1536]{2,1,0:T(8,128)(2,1)}, bf16[4,64,1536]{2,1,0:T(8,128)(2,1)}) async-done(((bf16[4,64,1536]{2,1,0:T(8,128)(2,1)}, bf16[4,64,1536]{2,1,0:T(8,128)(2,1)}), (bf16[4,64,1536]{2,1,0:T(8,128)(2,1)}, bf16[4,64,1536]{2,1,0:T(8,128)(2,1)})) %all-reduce.15.cloned.1.call-update) | async-done | bytes 1572880 | tf_op jit(solution)/shard_map/psum | solution.py:304
  735.5 18.1 %all-reduce.4 = (bf16[1536]{0:T(1024)(128)(2,1)S(1)}, bf16[1536]{0:T(1024)(128)(2,1)S(1)}) all-reduce(bf16[1536]{0:T(1024)(128)(2,1)S(1)} %get-tuple-element.1136, bf16[1536]{0:T(1024)(128)(2,1)S(1)} %copy-done.91), channel_id=2, replica_groups=mesh['fsdp'=2,'ctx'=4,'tp'=4] {'fsdp','ctx'}, use_global_device_ids=true, to_apply=%region_24.25.clone | all-reduce | flops 3072 | bytes 12288
  754.2 3.2 fusion.98
  757.5 15.4 %reduce-scatter.20.cloned.1.call-done = bf16[192,384]{1,0:T(8,128)(2,1)} async-done(((bf16[1536,384]{1,0:T(8,128)(2,1)}), bf16[192,384]{1,0:T(8,128)(2,1)}) %reduce-scatter.20.cloned.1.call-update) | async-done | bytes 147472 | tf_op jit(solution)/shard_map/reduce_scatter | solution.py:421
  774.5 35.5 %reduce-scatter.22.cloned.1.call-done = bf16[192,384]{1,0:T(8,128)(2,1)} async-done(((bf16[1536,384]{1,0:T(8,128)(2,1)}), bf16[192,384]{1,0:T(8,128)(2,1)}) %reduce-scatter.22.cloned.1.call-update) | async-done | bytes 147472 | tf_op jit(solution)/shard_map/reduce_scatter | solution.py:427
  811.6 36.3 %reduce-scatter.18.cloned.1.call-done = bf16[192,384]{1,0:T(8,128)(2,1)} async-done(((bf16[1536,384]{1,0:T(8,128)(2,1)}), bf16[192,384]{1,0:T(8,128)(2,1)}) %reduce-scatter.18.cloned.1.call-update) | async-done | bytes 147472 | tf_op jit(solution)/shard_map/reduce_scatter | solution.py:418
  849.5 36.2 %reduce-scatter.16.cloned.1.call-done = bf16[192,384]{1,0:T(8,128)(2,1)} async-done(((bf16[1536,384]{1,0:T(8,128)(2,1)}), bf16[192,384]{1,0:T(8,128)(2,1)}) %reduce-scatter.16.cloned.1.call-update) | async-done | bytes 147472 | tf_op jit(solution)/shard_map/reduce_scatter | solution.py:415
  887.4 36.2 %reduce-scatter.14.cloned.1.call-done = bf16[192,384]{1,0:T(8,128)(2,1)} async-done(((bf16[1536,384]{1,0:T(8,128)(2,1)}), bf16[192,384]{1,0:T(8,128)(2,1)}) %reduce-scatter.14.cloned.1.call-update) | async-done | bytes 147472 | tf_op jit(solution)/shard_map/reduce_scatter | solution.py:412
  925.2 68.8 %reduce-scatter.30.cloned.1.call-done = bf16[192,1024]{1,0:T(8,128)(2,1)} async-done(((bf16[1536,1024]{1,0:T(8,128)(2,1)}), bf16[192,1024]{1,0:T(8,128)(2,1)}) %reduce-scatter.30.cloned.1.call-update) | async-done | bytes 393232
  996.2 68.0 %reduce-scatter.24.cloned.1.call-done = bf16[192,1024]{1,0:T(8,128)(2,1)} async-done(((bf16[1536,1024]{1,0:T(8,128)(2,1)}), bf16[192,1024]{1,0:T(8,128)(2,1)}) %reduce-scatter.24.cloned.1.call-update) | async-done | bytes 393232 | tf_op jit(solution)/shard_map/reduce_scatter | solution.py:433
  1066.2 68.2 %reduce-scatter.26.cloned.1.call-done = bf16[192,1024]{1,0:T(8,128)(2,1)} async-done(((bf16[1536,1024]{1,0:T(8,128)(2,1)}), bf16[192,1024]{1,0:T(8,128)(2,1)}) %reduce-scatter.26.cloned.1.call-update) | async-done | bytes 393232 | tf_op jit(solution)/shard_map/reduce_scatter | solution.py:436
  (489 shorter events, 194.3 us)
Async XLA Ops:
  7.2 51.6 %copy-start.20 = (bf16[4,64,1536]{2,1,0:T(8,128)(2,1)S(1)}, bf16[4,64,1536]{2,1,0:T(8,128)(2,1)}, u32[]{:S(2)}) copy-start(bf16[4,64,1536]{2,1,0:T(8,128)(2,1)} %param.21) | copy-start | bytes 2359300
  7.2 29.5 %copy-start.93 = (bf16[192,3]{0,1:T(4,128)(2,1)S(1)}, bf16[192,3]{0,1:T(4,128)(2,1)}, u32[]{:S(2)}) copy-start(bf16[192,3]{0,1:T(4,128)(2,1)} %param.29) | copy-start | bytes 3460
  7.2 54.5 %all-gather.14.cloned.1.call-start = ((), (), s32[]{:S(2)}) async-start(), calls=%async_computation.11 | async-start | bytes 1327104 | tf_op jit(solution)/shard_map/all_gather | solution.py:127
  7.9 51.4 %copy-start.87 = (s32[4,64]{1,0:T(4,128)S(1)}, s32[4,64]{1,0:T(4,128)}, u32[]{:S(2)}) copy-start(s32[4,64]{1,0:T(4,128)} %param.22) | copy-start | bytes 3076
  7.9 55.9 %all-gather.12.cloned.1.call-start = ((), (), s32[]{:S(2)}) async-start(), calls=%async_computation.10 | async-start | bytes 1327104 | tf_op jit(solution)/shard_map/all_gather | solution.py:125
  8.7 51.0 %copy-start.94 = (s32[4,1]{0,1:T(1,128)S(1)}, s32[4,1]{0,1:T(1,128)}, u32[]{:S(2)}) copy-start(s32[4,1]{0,1:T(1,128)} %param.23) | copy-start | bytes 52
  8.7 75.2 %all-gather.10.cloned.1.call-start = ((), (), s32[]{:S(2)}) async-start(), calls=%async_computation.9 | async-start | bytes 1327104 | tf_op jit(solution)/shard_map/all_gather | solution.py:124
  9.4 147.4 %all-gather.16.cloned.1.call-start = ((), (), s32[]{:S(2)}) async-start(), calls=%async_computation.12 | async-start | bytes 1327104 | tf_op jit(solution)/shard_map/all_gather | solution.py:126
  10.0 243.3 %all-gather.18.cloned.1.call-start = ((), (), s32[]{:S(2)}) async-start(), calls=%async_computation.13 | async-start | bytes 1327104 | tf_op jit(solution)/shard_map/all_gather | solution.py:129
  10.6 307.9 %all-reduce.11.cloned.1.call-start = ((), (), s32[]{:S(2)}) async-start(), calls=%async_computation.14 | async-start | bytes 3145728 | tf_op jit(solution)/shard_map/psum | solution.py:295
  10.7 79.0 %copy-start.67 = (pred[64,64]{1,0:T(8,128)(4,1)}, pred[64,64]{1,0:T(8,128)(4,1)S(1)}, u32[]{:S(2)}) copy-start(pred[64,64]{1,0:T(8,128)(4,1)S(1)} %iota_compare_fusion.2) | copy-start | bytes 12292
  10.7 79.0 %copy-start.69 = (pred[64,64]{1,0:T(8,128)(4,1)}, pred[64,64]{1,0:T(8,128)(4,1)S(1)}, u32[]{:S(2)}) copy-start(pred[64,64]{1,0:T(8,128)(4,1)S(1)} %iota_compare_fusion.3) | copy-start | bytes 12292
  10.7 79.0 %copy-start.82 = (pred[64,64]{1,0:T(8,128)(4,1)}, pred[64,64]{1,0:T(8,128)(4,1)S(1)}, u32[]{:S(2)}) copy-start(pred[64,64]{1,0:T(8,128)(4,1)S(1)} %iota_compare_fusion.1) | copy-start | bytes 12292
  35.3 121.6 %copy-start.73 = (f32[1536]{0:T(1024)}, f32[1536]{0:T(1024)S(1)}, u32[]{:S(2)}) copy-start(f32[1536]{0:T(1024)S(1)} %convert_element_type.291) | copy-start | bytes 18436
  36.7 120.2 %copy-start.88 = (f32[4,64]{1,0:T(4,128)}, f32[4,64]{1,0:T(4,128)S(1)}, u32[]{:S(2)}) copy-start(f32[4,64]{1,0:T(4,128)S(1)} %add_rsqrt_fusion.2) | copy-start | bytes 3076
  66.5 22.4 %copy-start.31 = (f32[4,64,3,128]{3,2,1,0:T(4,128)}, f32[4,64,3,128]{3,2,1,0:T(4,128)S(1)}, u32[]{:S(2)}) copy-start(f32[4,64,3,128]{3,2,1,0:T(4,128)S(1)} %reshape.183) | copy-start | bytes 1179652
  85.8 70.4 %copy-start.23 = (f32[4,8,3,8,128]{4,3,2,1,0:T(8,128)}, f32[4,8,3,8,128]{4,3,2,1,0:T(8,128)S(1)}, u32[]{:S(2)}) copy-start(f32[4,8,3,8,128]{4,3,2,1,0:T(8,128)S(1)} %convolution_bitcast_fusion.9) | copy-start | bytes 1179652
  89.7 64.3 %copy-start.27 = (f32[4,3,64,64]{3,2,1,0:T(8,128)}, f32[4,3,64,64]{3,2,1,0:T(8,128)S(1)}, u32[]{:S(2)}) copy-start(f32[4,3,64,64]{3,2,1,0:T(8,128)S(1)} %convolution_select_fusion.1) | copy-start | bytes 589828
  89.8 63.8 %copy-start.43 = (f32[4,3,64,64]{3,2,1,0:T(8,128)S(1)}, f32[4,3,64,64]{3,2,1,0:T(8,128)}, u32[]{:S(2)}) copy-start(f32[4,3,64,64]{3,2,1,0:T(8,128)} %convolution_select_fusion.3) | copy-start | bytes 589828
  159.0 84.3 %copy-start.36 = (bf16[4,3,64,128]{3,2,1,0:T(8,128)(2,1)}, bf16[4,3,64,128]{3,2,1,0:T(8,128)(2,1)S(1)}, u32[]{:S(2)}) copy-start(bf16[4,3,64,128]{3,2,1,0:T(8,128)(2,1)S(1)} %copy.186) | copy-start | bytes 589828
  161.5 81.8 %copy-start.13 = (f32[4,3,64,64]{2,3,1,0:T(8,128)}, f32[4,3,64,64]{2,3,1,0:T(8,128)S(1)}, u32[]{:S(2)}) copy-start(f32[4,3,64,64]{2,3,1,0:T(8,128)S(1)} %get-tuple-element.1238) | copy-start | bytes 589828
  164.6 22.3 %collective-permute-start.2 = (bf16[4,3,128,128]{3,2,1,0:T(8,128)(2,1)}, bf16[4,3,128,128]{3,2,1,0:T(8,128)(2,1)S(1)}, u32[]{:S(2)}, u32[]{:S(2)}) collective-permute-start(bf16[4,3,128,128]{3,2,1,0:T(8,128)(2,1)} %get-tuple-element.1517), channel_id=1, source_target_pairs={{0,4},{4,8},{8,12},{1,5},{5,9},{9,13},{2,6},{6,10},{10,14},{3,7},{... | collective-permute-start | bytes 1179656 | tf_op jit(solution)/shard_map/while/body/eval_jaxpr/ppermute | solution.py:16
  168.0 13.9 %collective-permute-start = (bf16[4,3,64,128]{3,2,1,0:T(8,128)(2,1)}, bf16[4,3,64,128]{3,2,1,0:T(8,128)(2,1)S(1)}, u32[]{:S(2)}, u32[]{:S(2)}) collective-permute-start(bf16[4,3,64,128]{3,2,1,0:T(8,128)(2,1)} %get-tuple-element.1515), channel_id=1, source_target_pairs={{0,4},{4,8},{8,12},{1,5},{5,9},{9,13},{2,6},{6,10},{10,14},{3,7},{... | collective-permute-start | bytes 589832 | tf_op jit(solution)/shard_map/while/body/eval_jaxpr/ppermute | solution.py:16
  171.0 14.4 %collective-permute-start.1 = (bf16[4,3,64,128]{3,2,1,0:T(8,128)(2,1)}, bf16[4,3,64,128]{3,2,1,0:T(8,128)(2,1)S(1)}, u32[]{:S(2)}, u32[]{:S(2)}) collective-permute-start(bf16[4,3,64,128]{3,2,1,0:T(8,128)(2,1)} %get-tuple-element.1516), channel_id=1, source_target_pairs={{0,4},{4,8},{8,12},{1,5},{5,9},{9,13},{2,6},{6,10},{10,14},{3,7},{... | collective-permute-start | bytes 589832 | tf_op jit(solution)/shard_map/while/body/eval_jaxpr/ppermute | solution.py:16
  190.6 22.4 %collective-permute-start.2 = (bf16[4,3,128,128]{3,2,1,0:T(8,128)(2,1)}, bf16[4,3,128,128]{3,2,1,0:T(8,128)(2,1)S(1)}, u32[]{:S(2)}, u32[]{:S(2)}) collective-permute-start(bf16[4,3,128,128]{3,2,1,0:T(8,128)(2,1)} %get-tuple-element.1517), channel_id=1, source_target_pairs={{0,4},{4,8},{8,12},{1,5},{5,9},{9,13},{2,6},{6,10},{10,14},{3,7},{... | collective-permute-start | bytes 1179656 | tf_op jit(solution)/shard_map/while/body/eval_jaxpr/ppermute | solution.py:16
  194.9 14.1 %collective-permute-start = (bf16[4,3,64,128]{3,2,1,0:T(8,128)(2,1)}, bf16[4,3,64,128]{3,2,1,0:T(8,128)(2,1)S(1)}, u32[]{:S(2)}, u32[]{:S(2)}) collective-permute-start(bf16[4,3,64,128]{3,2,1,0:T(8,128)(2,1)} %get-tuple-element.1515), channel_id=1, source_target_pairs={{0,4},{4,8},{8,12},{1,5},{5,9},{9,13},{2,6},{6,10},{10,14},{3,7},{... | collective-permute-start | bytes 589832 | tf_op jit(solution)/shard_map/while/body/eval_jaxpr/ppermute | solution.py:16
  198.0 13.6 %collective-permute-start.1 = (bf16[4,3,64,128]{3,2,1,0:T(8,128)(2,1)}, bf16[4,3,64,128]{3,2,1,0:T(8,128)(2,1)S(1)}, u32[]{:S(2)}, u32[]{:S(2)}) collective-permute-start(bf16[4,3,64,128]{3,2,1,0:T(8,128)(2,1)} %get-tuple-element.1516), channel_id=1, source_target_pairs={{0,4},{4,8},{8,12},{1,5},{5,9},{9,13},{2,6},{6,10},{10,14},{3,7},{... | collective-permute-start | bytes 589832 | tf_op jit(solution)/shard_map/while/body/eval_jaxpr/ppermute | solution.py:16
  216.8 21.5 %collective-permute-start.2 = (bf16[4,3,128,128]{3,2,1,0:T(8,128)(2,1)}, bf16[4,3,128,128]{3,2,1,0:T(8,128)(2,1)S(1)}, u32[]{:S(2)}, u32[]{:S(2)}) collective-permute-start(bf16[4,3,128,128]{3,2,1,0:T(8,128)(2,1)} %get-tuple-element.1517), channel_id=1, source_target_pairs={{0,4},{4,8},{8,12},{1,5},{5,9},{9,13},{2,6},{6,10},{10,14},{3,7},{... | collective-permute-start | bytes 1179656 | tf_op jit(solution)/shard_map/while/body/eval_jaxpr/ppermute | solution.py:16
  221.1 13.7 %collective-permute-start = (bf16[4,3,64,128]{3,2,1,0:T(8,128)(2,1)}, bf16[4,3,64,128]{3,2,1,0:T(8,128)(2,1)S(1)}, u32[]{:S(2)}, u32[]{:S(2)}) collective-permute-start(bf16[4,3,64,128]{3,2,1,0:T(8,128)(2,1)} %get-tuple-element.1515), channel_id=1, source_target_pairs={{0,4},{4,8},{8,12},{1,5},{5,9},{9,13},{2,6},{6,10},{10,14},{3,7},{... | collective-permute-start | bytes 589832 | tf_op jit(solution)/shard_map/while/body/eval_jaxpr/ppermute | solution.py:16
  224.1 12.7 %collective-permute-start.1 = (bf16[4,3,64,128]{3,2,1,0:T(8,128)(2,1)}, bf16[4,3,64,128]{3,2,1,0:T(8,128)(2,1)S(1)}, u32[]{:S(2)}, u32[]{:S(2)}) collective-permute-start(bf16[4,3,64,128]{3,2,1,0:T(8,128)(2,1)} %get-tuple-element.1516), channel_id=1, source_target_pairs={{0,4},{4,8},{8,12},{1,5},{5,9},{9,13},{2,6},{6,10},{10,14},{3,7},{... | collective-permute-start | bytes 589832 | tf_op jit(solution)/shard_map/while/body/eval_jaxpr/ppermute | solution.py:16
  253.3 257.7 %copy-start.7 = (f32[4,3,64,128]{3,2,1,0:T(8,128)}, f32[4,3,64,128]{3,2,1,0:T(8,128)S(1)}, u32[]{:S(2)}) copy-start(f32[4,3,64,128]{3,2,1,0:T(8,128)S(1)} %get-tuple-element.859) | copy-start | bytes 1179652
  256.8 61.7 %copy-start.21 = (bf16[4,64,1536]{2,1,0:T(8,128)(2,1)S(1)}, bf16[4,64,1536]{2,1,0:T(8,128)(2,1)}, u32[]{:S(2)}) copy-start(bf16[4,64,1536]{2,1,0:T(8,128)(2,1)} %param.21) | copy-start | bytes 2359300
  256.9 101.7 %all-gather.22.cloned.1.call-start = ((), (), s32[]{:S(2)}) async-start(), calls=%async_computation.16 | async-start | bytes 3538944 | tf_op jit(solution)/shard_map/all_gather | solution.py:132
  257.6 139.8 %all-gather.24.cloned.1.call-start = ((), (), s32[]{:S(2)}) async-start(), calls=%async_computation.17 | async-start | bytes 3538944 | tf_op jit(solution)/shard_map/all_gather | solution.py:133
  258.4 177.9 %all-gather.20.cloned.1.call-start = ((), (), s32[]{:S(2)}) async-start(), calls=%async_computation.15 | async-start | bytes 3538944 | tf_op jit(solution)/shard_map/all_gather | solution.py:131
  259.1 246.7 %all-reduce.13.cloned.1.call-start = ((), (), s32[]{:S(2)}) async-start(), calls=%async_computation.18 | async-start | bytes 3145728 | tf_op jit(solution)/shard_map/psum | solution.py:316
  321.9 75.5 %copy-start.59 = (bf16[4,64,1536]{2,1,0:T(8,128)(2,1)S(1)}, bf16[4,64,1536]{2,1,0:T(8,128)(2,1)}, u32[]{:S(2)}) copy-start(bf16[4,64,1536]{2,1,0:T(8,128)(2,1)} %param.35) | copy-start | bytes 2359300
  445.9 231.3 %reduce-scatter.28.cloned.1.call-start = ((), (), s32[]{:S(2)}) async-start(), calls=%async_computation.26 | async-start | bytes 442368
  519.5 6.7 copy-start.9
  519.5 6.7 copy-start.16
  521.8 23.2 %collective-permute-start.5 = (bf16[4,3,128,128]{2,3,1,0:T(8,128)(2,1)}, bf16[4,3,128,128]{2,3,1,0:T(8,128)(2,1)}, u32[]{:S(2)}, u32[]{:S(2)}) collective-permute-start(bf16[4,3,128,128]{2,3,1,0:T(8,128)(2,1)} %fusion.412), channel_id=1, source_target_pairs={{4,0},{8,4},{12,8},{5,1},{9,5},{13,9},{6,2},{10,6},{14,10},{7,3},{... | collective-permute-start | bytes 1179656 | tf_op jit(solution)/shard_map/while/body/eval_jaxpr/ppermute | solution.py:16
  524.9 15.2 %collective-permute-start.3 = (bf16[4,3,64,128]{3,2,1,0:T(8,128)(2,1)}, bf16[4,3,64,128]{3,2,1,0:T(8,128)(2,1)}, u32[]{:S(2)}, u32[]{:S(2)}) collective-permute-start(bf16[4,3,64,128]{3,2,1,0:T(8,128)(2,1)} %fusion.409), channel_id=1, source_target_pairs={{4,0},{8,4},{12,8},{5,1},{9,5},{13,9},{6,2},{10,6},{14,10},{7,3},{... | collective-permute-start | bytes 589832 | tf_op jit(solution)/shard_map/while/body/eval_jaxpr/ppermute | solution.py:16
  527.2 16.1 %collective-permute-start.4 = (bf16[4,3,64,128]{3,2,1,0:T(8,128)(2,1)}, bf16[4,3,64,128]{3,2,1,0:T(8,128)(2,1)}, u32[]{:S(2)}, u32[]{:S(2)}) collective-permute-start(bf16[4,3,64,128]{3,2,1,0:T(8,128)(2,1)} %fusion.410), channel_id=1, source_target_pairs={{4,0},{8,4},{12,8},{5,1},{9,5},{13,9},{6,2},{10,6},{14,10},{7,3},{... | collective-permute-start | bytes 589832 | tf_op jit(solution)/shard_map/while/body/eval_jaxpr/ppermute | solution.py:16
  552.4 6.7 copy-start.9
  552.4 6.7 copy-start.16
  554.6 22.3 %collective-permute-start.5 = (bf16[4,3,128,128]{2,3,1,0:T(8,128)(2,1)}, bf16[4,3,128,128]{2,3,1,0:T(8,128)(2,1)}, u32[]{:S(2)}, u32[]{:S(2)}) collective-permute-start(bf16[4,3,128,128]{2,3,1,0:T(8,128)(2,1)} %fusion.412), channel_id=1, source_target_pairs={{4,0},{8,4},{12,8},{5,1},{9,5},{13,9},{6,2},{10,6},{14,10},{7,3},{... | collective-permute-start | bytes 1179656 | tf_op jit(solution)/shard_map/while/body/eval_jaxpr/ppermute | solution.py:16
  557.8 15.3 %collective-permute-start.3 = (bf16[4,3,64,128]{3,2,1,0:T(8,128)(2,1)}, bf16[4,3,64,128]{3,2,1,0:T(8,128)(2,1)}, u32[]{:S(2)}, u32[]{:S(2)}) collective-permute-start(bf16[4,3,64,128]{3,2,1,0:T(8,128)(2,1)} %fusion.409), channel_id=1, source_target_pairs={{4,0},{8,4},{12,8},{5,1},{9,5},{13,9},{6,2},{10,6},{14,10},{7,3},{... | collective-permute-start | bytes 589832 | tf_op jit(solution)/shard_map/while/body/eval_jaxpr/ppermute | solution.py:16
  560.0 15.2 %collective-permute-start.4 = (bf16[4,3,64,128]{3,2,1,0:T(8,128)(2,1)}, bf16[4,3,64,128]{3,2,1,0:T(8,128)(2,1)}, u32[]{:S(2)}, u32[]{:S(2)}) collective-permute-start(bf16[4,3,64,128]{3,2,1,0:T(8,128)(2,1)} %fusion.410), channel_id=1, source_target_pairs={{4,0},{8,4},{12,8},{5,1},{9,5},{13,9},{6,2},{10,6},{14,10},{7,3},{... | collective-permute-start | bytes 589832 | tf_op jit(solution)/shard_map/while/body/eval_jaxpr/ppermute | solution.py:16
  584.4 6.7 copy-start.9
  584.4 6.7 copy-start.16
  586.6 21.4 %collective-permute-start.5 = (bf16[4,3,128,128]{2,3,1,0:T(8,128)(2,1)}, bf16[4,3,128,128]{2,3,1,0:T(8,128)(2,1)}, u32[]{:S(2)}, u32[]{:S(2)}) collective-permute-start(bf16[4,3,128,128]{2,3,1,0:T(8,128)(2,1)} %fusion.412), channel_id=1, source_target_pairs={{4,0},{8,4},{12,8},{5,1},{9,5},{13,9},{6,2},{10,6},{14,10},{7,3},{... | collective-permute-start | bytes 1179656 | tf_op jit(solution)/shard_map/while/body/eval_jaxpr/ppermute | solution.py:16
  589.8 14.4 %collective-permute-start.3 = (bf16[4,3,64,128]{3,2,1,0:T(8,128)(2,1)}, bf16[4,3,64,128]{3,2,1,0:T(8,128)(2,1)}, u32[]{:S(2)}, u32[]{:S(2)}) collective-permute-start(bf16[4,3,64,128]{3,2,1,0:T(8,128)(2,1)} %fusion.409), channel_id=1, source_target_pairs={{4,0},{8,4},{12,8},{5,1},{9,5},{13,9},{6,2},{10,6},{14,10},{7,3},{... | collective-permute-start | bytes 589832 | tf_op jit(solution)/shard_map/while/body/eval_jaxpr/ppermute | solution.py:16
  592.0 14.3 %collective-permute-start.4 = (bf16[4,3,64,128]{3,2,1,0:T(8,128)(2,1)}, bf16[4,3,64,128]{3,2,1,0:T(8,128)(2,1)}, u32[]{:S(2)}, u32[]{:S(2)}) collective-permute-start(bf16[4,3,64,128]{3,2,1,0:T(8,128)(2,1)} %fusion.410), channel_id=1, source_target_pairs={{4,0},{8,4},{12,8},{5,1},{9,5},{13,9},{6,2},{10,6},{14,10},{7,3},{... | collective-permute-start | bytes 589832 | tf_op jit(solution)/shard_map/while/body/eval_jaxpr/ppermute | solution.py:16
  618.8 16.6 %copy-start.77 = (f32[4,3,64]{2,1,0:T(4,128)}, f32[4,3,64]{2,1,0:T(4,128)S(1)}, u32[]{:S(2)}) copy-start(f32[4,3,64]{2,1,0:T(4,128)S(1)} %get-tuple-element.1241) | copy-start | bytes 9220
  638.1 95.4 %all-reduce.15.cloned.1.call-start = ((), (), s32[]{:S(2)}) async-start(), calls=%async_computation.28 | async-start | bytes 3145728 | tf_op jit(solution)/shard_map/psum | solution.py:304
  645.5 127.3 %reduce-scatter.20.cloned.1.call-start = ((), (), s32[]{:S(2)}) async-start(), calls=%async_computation.22 | async-start | bytes 1327104 | tf_op jit(solution)/shard_map/reduce_scatter | solution.py:421
  648.6 161.4 %reduce-scatter.22.cloned.1.call-start = ((), (), s32[]{:S(2)}) async-start(), calls=%async_computation.23 | async-start | bytes 1327104 | tf_op jit(solution)/shard_map/reduce_scatter | solution.py:427
  650.4 197.5 %reduce-scatter.18.cloned.1.call-start = ((), (), s32[]{:S(2)}) async-start(), calls=%async_computation.21 | async-start | bytes 1327104 | tf_op jit(solution)/shard_map/reduce_scatter | solution.py:418
  653.4 232.3 %reduce-scatter.16.cloned.1.call-start = ((), (), s32[]{:S(2)}) async-start(), calls=%async_computation.20 | async-start | bytes 1327104 | tf_op jit(solution)/shard_map/reduce_scatter | solution.py:415
  656.3 267.2 %reduce-scatter.14.cloned.1.call-start = ((), (), s32[]{:S(2)}) async-start(), calls=%async_computation.19 | async-start | bytes 1327104 | tf_op jit(solution)/shard_map/reduce_scatter | solution.py:412
  659.6 334.3 %reduce-scatter.30.cloned.1.call-start = ((), (), s32[]{:S(2)}) async-start(), calls=%async_computation.27 | async-start | bytes 3538944
  668.3 396.0 %reduce-scatter.24.cloned.1.call-start = ((), (), s32[]{:S(2)}) async-start(), calls=%async_computation.24 | async-start | bytes 3538944 | tf_op jit(solution)/shard_map/reduce_scatter | solution.py:433
  672.4 462.1 %reduce-scatter.26.cloned.1.call-start = ((), (), s32[]{:S(2)}) async-start(), calls=%async_computation.25 | async-start | bytes 3538944 | tf_op jit(solution)/shard_map/reduce_scatter | solution.py:436
  676.5 59.0 %copy-start.91 = (bf16[1536]{0:T(1024)(128)(2,1)S(1)}, bf16[1536]{0:T(1024)(128)(2,1)}, u32[]{:S(2)}) copy-start(bf16[1536]{0:T(1024)(128)(2,1)} %get-tuple-element.1134) | copy-start | bytes 9220
  (81 other events, 195.5 us)
Sparse Core Ops, SparseCore 0:
  9.6 26.0 all-gather.13
  37.3 22.6 all-gather.11
  61.6 22.2 all-gather.9
  85.4 22.5 all-gather.15
  109.4 22.7 all-gather.17
  257.0 61.4 all-reduce.10
  320.2 38.2 all-gather.21
  360.2 37.1 all-gather.23
  399.1 37.1 all-gather.19
  446.0 59.7 all-reduce.12
  638.3 31.5 reduce-scatter.27
  673.7 59.8 all-reduce.14
  735.8 36.9 reduce-scatter.19
  775.0 34.9 reduce-scatter.21
  812.1 35.7 reduce-scatter.17
  850.0 35.6 reduce-scatter.15
  887.8 35.6 reduce-scatter.13
  925.7 68.2 reduce-scatter.29
  996.3 67.9 reduce-scatter.23
  1066.4 67.9 reduce-scatter.25
where the time goes:
time: 1150 us; the launch traced here: 1140 us
  waiting for transfers between devices  706 us (61%)
  matrix products  171 us (15%)
  other arithmetic  117 us (10%)
  blocking collectives  60.2 us (5%)
  starting transfers between devices  41.9 us (4%)
  local copies, waits for them, and re-layouts  28.9 us (3%)
  between operations  17.5 us (2%)
    unnamed x22, waiting for transfers between devices  74.2 us
    reduce_scatter x1, waiting for transfers between devices, shards(): lax.psum_scatter(up_grad.astype(jnp.bfloat16), ('fsdp', 'ctx'), scatter_d...  68.2 us
    reduce_scatter x1, waiting for transfers between devices, shards(): lax.psum_scatter(gate_grad.astype(jnp.bfloat16), ('fsdp', 'ctx'), scatter...  68 us
    another operation x1, other arithmetic, group_algebra(): inverse = jax.scipy.linalg.solve_triangular(system, identity, lower=True)  59.9 us
    psum x1, waiting for transfers between devices, shards(): branch = lax.psum(project_back(attn_low, out_full), 'tp')  58.9 us
    psum x1, waiting for transfers between devices, shards(): lax.psum(project_back(hidden_low, down_full).astype(jnp.bfloat16), 'tp')  54.9 us
    psum x1, waiting for transfers between devices, shards(): lax.psum(project_back(d_gate, gate_full) + project_back(d_up, up_full), '...  53.5 us
    ppermute x18, waiting for transfers between devices, passed_along(): return lax.ppermute(block, axis, route)  45 us
  transfers between devices with their start and end apart: 38, of which 27 were waited for; matrix products, arithmetic and copies ran while one was open for 21% of the time, Pallas kernels for 0%

commit v1 on v0

--- a/solution.py
+++ b/solution.py
@@ -50,11 +50,15 @@
 
 
 def doc_starts_local(segment_ids, group_first, first_position):
+    length = segment_ids.shape[-1]
+    previous = jnp.concatenate([segment_ids[..., :1], segment_ids[..., :-1]], axis=-1)
     offsets = lax.broadcasted_iota(jnp.int32, segment_ids.shape, segment_ids.ndim - 1)
-    previous = jnp.concatenate([segment_ids[..., :1], segment_ids[..., :-1]], axis=-1)
     boundary = (offsets > 0) & (segment_ids != previous)
     marks = jnp.where(boundary, offsets + first_position, -1)
-    return jnp.maximum(lax.cummax(marks, axis=segment_ids.ndim - 1), group_first)
+    row_index = lax.broadcasted_iota(jnp.int32, (length, length), 0)
+    column_index = lax.broadcasted_iota(jnp.int32, (length, length), 1)
+    seen = jnp.where(column_index <= row_index, marks[..., None, :], -1)
+    return jnp.maximum(jnp.max(seen, axis=-1), group_first)
 
 
 def norm_rows(values):
@@ -404,41 +408,24 @@
     input_grad = (d_middle + norm_back(d_one, normed_one, factor_one, gain_one_f)).astype(
         jnp.bfloat16
     )
+
+    def scattered(partial):
+        first = lax.psum_scatter(partial, "fsdp", scatter_dimension=0, tiled=True)
+        return lax.psum_scatter(first, "ctx", scatter_dimension=0, tiled=True)
+
     results = tuple(
         (
-            lax.psum_scatter(
-                gain_one_grad.astype(jnp.bfloat16), ("fsdp", "ctx"), scatter_dimension=0, tiled=True
-            ).astype(jnp.float32),
-            lax.psum_scatter(
-                query_grad.astype(jnp.bfloat16), ("fsdp", "ctx"), scatter_dimension=0, tiled=True
-            ).astype(jnp.float32),
-            lax.psum_scatter(
-                key_grad.astype(jnp.bfloat16), ("fsdp", "ctx"), scatter_dimension=0, tiled=True
-            ).astype(jnp.float32),
-            lax.psum_scatter(
-                value_grad.astype(jnp.bfloat16), ("fsdp", "ctx"), scatter_dimension=0, tiled=True
-            ).astype(jnp.float32),
-            lax.psum_scatter(
-                house_grad.astype(jnp.bfloat16), ("fsdp", "ctx"), scatter_dimension=0, tiled=True
-            ).astype(jnp.float32),
-            lax.psum_scatter(
-                beta_grad.astype(jnp.bfloat16), ("fsdp", "ctx"), scatter_dimension=0, tiled=True
-            ).astype(jnp.float32),
-            lax.psum_scatter(
-                out_grad.astype(jnp.bfloat16), ("fsdp", "ctx"), scatter_dimension=0, tiled=True
-            ).astype(jnp.float32),
-            lax.psum_scatter(
-                gain_two_grad.astype(jnp.bfloat16), ("fsdp", "ctx"), scatter_dimension=0, tiled=True
-            ).astype(jnp.float32),
-            lax.psum_scatter(
-                gate_grad.astype(jnp.bfloat16), ("fsdp", "ctx"), scatter_dimension=0, tiled=True
-            ).astype(jnp.float32),
-            lax.psum_scatter(
-                up_grad.astype(jnp.bfloat16), ("fsdp", "ctx"), scatter_dimension=0, tiled=True
-            ).astype(jnp.float32),
-            lax.psum_scatter(
-                down_grad.astype(jnp.bfloat16), ("fsdp", "ctx"), scatter_dimension=0, tiled=True
-            ).astype(jnp.float32),
+            scattered(gain_one_grad.astype(jnp.bfloat16)).astype(jnp.float32),
+            scattered(query_grad.astype(jnp.bfloat16)).astype(jnp.float32),
+            scattered(key_grad.astype(jnp.bfloat16)).astype(jnp.float32),
+            scattered(value_grad.astype(jnp.bfloat16)).astype(jnp.float32),
+            scattered(house_grad.astype(jnp.bfloat16)).astype(jnp.float32),
+            scattered(beta_grad.astype(jnp.bfloat16)).astype(jnp.float32),
+            scattered(out_grad.astype(jnp.bfloat16)).astype(jnp.float32),
+            scattered(gain_two_grad.astype(jnp.bfloat16)).astype(jnp.float32),
+            scattered(gate_grad.astype(jnp.bfloat16)).astype(jnp.float32),
+            scattered(up_grad.astype(jnp.bfloat16)).astype(jnp.float32),
+            scattered(down_grad.astype(jnp.bfloat16)).astype(jnp.float32),
         )
     )
     return (block_out, input_grad) + results

time: 1150 us -> 1070 us (0.930)
  waiting for transfers between devices: 706 us -> 619 us
    reduce_scatter x7 -> x15, waiting for transfers between devices: 296 us -> 210 us  [the longest x7 157 us: scattered(): return lax.psum_scatter(first, 'ctx', scatter_dimension=0, tiled=True)]
    unnamed x22 -> x32, waiting for transfers between devices: 74.2 us -> 61.9 us
    unnamed x2 -> x3, blocking collectives: 38.3 us -> 34.8 us
    unnamed x192 -> x258, local copies, waits for them, and re-layouts: 20.9 us -> 24.2 us
  transfers between devices with their start and end apart: 38 -> 47, of which waited for: 27 -> 33; matrix products, arithmetic and copies ran while one was open for 21% -> 23% of each run, Pallas kernels for 0% -> 0%
where the time goes in v1:
time: 1070 us; the launch traced here: 1060 us
  waiting for transfers between devices  619 us (58%)
  matrix products  177 us (17%)
  other arithmetic  115 us (11%)
  blocking collectives  56.7 us (5%)
  starting transfers between devices  42.4 us (4%)
  local copies, waits for them, and re-layouts  32.2 us (3%)
  between operations  18.3 us (2%)
    reduce_scatter x7, waiting for transfers between devices, scattered(): return lax.psum_scatter(first, 'ctx', scatter_dimension=0, tiled=True)  157 us
    unnamed x32, waiting for transfers between devices  61.9 us
    psum x1, waiting for transfers between devices, shards(): lax.psum(project_back(hidden_low, down_full).astype(jnp.bfloat16), 'tp')  61.5 us
    another operation x1, other arithmetic, group_algebra(): inverse = jax.scipy.linalg.solve_triangular(system, identity, lower=True)  59.8 us
    psum x1, waiting for transfers between devices, shards(): branch = lax.psum(project_back(attn_low, out_full), 'tp')  58.9 us
    psum x1, waiting for transfers between devices, shards(): lax.psum(project_back(d_gate, gate_full) + project_back(d_up, up_full), '...  57.5 us
    reduce_scatter x8, waiting for transfers between devices, scattered(): first = lax.psum_scatter(partial, 'fsdp', scatter_dimension=0, tiled=True)  52.8 us
    ppermute x18, waiting for transfers between devices, passed_along(): return lax.ppermute(block, axis, route)  45.1 us
  transfers between devices with their start and end apart: 47, of which 33 were waited for; matrix products, arithmetic and copies ran while one was open for 23% of the time, Pallas kernels for 0%

profile of v1, /device:TPU:0, one launch (start us, length us, event | category | flops | bytes accessed | tf_op | source)
XLA Modules:
  0.0 1061.5 jit_solution(1175647772940994881)
XLA Ops:
  15.0 20.3 %all-reduce.6 = (bf16[1536]{0:T(1024)(128)(2,1)S(1)}, bf16[1536]{0:T(1024)(128)(2,1)}) all-reduce(bf16[1536]{0:T(1024)(128)(2,1)S(1)} %dynamic-update-slice, bf16[1536]{0:T(1024)(128)(2,1)S(1)} %dynamic-update-slice.1), channel_id=1, replica_groups=mesh['fsdp'=2,'ctx'=4,'tp'=4] {'fsdp','ctx'}, use_global_device_ids=true, to_apply=%add | all-reduce | flops 3072 | bytes 12288
  36.7 21.9 %all-gather = bf16[8,192,3]{1,2,0:T(4,128)(2,1)S(1)} all-gather(bf16[1,192,3]{1,2,0:T(4,128)(2,1)S(1)} %bitcast.473), channel_id=1, replica_groups=mesh['fsdp'=2,'ctx'=4,'tp'=4] {'fsdp','ctx'}, dimensions={0}, use_global_device_ids=true | all-gather | bytes 10368 | tf_op jit(solution)/shard_map/all_gather | solution.py:132
  66.4 17.5 %all-gather.10.cloned.1.call-done = bf16[1536,384]{1,0:T(8,128)(2,1)} async-done(((bf16[192,384]{1,0:T(8,128)(2,1)}), bf16[1536,384]{1,0:T(8,128)(2,1)}) %all-gather.10.cloned.1.call-update) | async-done | bytes 1179664 | tf_op jit(solution)/shard_map/all_gather | solution.py:128
  90.7 59.8 %custom-call.7 = f32[4,3,1,64,64]{3,4,2,1,0:T(8,128)} custom-call(f32[4,3,1,64,64]{4,3,2,1,0:T(8,128)S(1)} %fusion.117), custom_call_target="InvertDiagBlocksLowerTriangular" | custom-call | tf_op jit(solution)/shard_map/jvp(vmap(vmap(jit(_solve_triangular))))/triangular_solve | solution.py:28
  164.7 77.5 %while.70 = (s32[]{:T(128)}, bf16[4,3,64,128]{3,2,1,0:T(8,128)(2,1)}, bf16[4,3,64,128]{3,2,1,0:T(8,128)(2,1)}, bf16[4,3,128,128]{3,2,1,0:T(8,128)(2,1)}, bf16[3,...) while((s32[]{:T(128)}, ...), condition=%wide.region_8.9_spmd.clone, body=%wide.region_5.8_spmd.clone.sunk | while | flops 466126400 | bytes 9536377 | solution.py:238
  164.7 3.4 collective-permute-start.2
  168.1 3.1 collective-permute-start
  171.2 2.6 collective-permute-start.1
  174.6 7.5 collective-permute-done
  182.7 2.9 collective-permute-done.1
  190.8 4.3 collective-permute-start.2
  195.1 3.0 collective-permute-start
  198.1 2.6 collective-permute-start.1
  201.5 7.6 collective-permute-done
  216.9 4.3 collective-permute-start.2
  221.2 3.1 collective-permute-start
  224.3 2.5 collective-permute-start.1
  227.6 7.3 collective-permute-done
  245.8 7.6 while.71
  253.5 3.5 fusion.120
  259.7 58.9 %all-reduce.14.cloned.1.call-done = f32[4,64,1536]{2,1,0:T(8,128)} async-done(((f32[4,64,1536]{2,1,0:T(8,128)}), f32[4,64,1536]{2,1,0:T(8,128)}) %all-reduce.14.cloned.1.call-update) | async-done | bytes 1572880 | tf_op jit(solution)/shard_map/psum | solution.py:299
  322.0 36.6 %all-gather.22.cloned.1.call-done = bf16[1536,1024]{1,0:T(8,128)(2,1)} async-done(((bf16[192,1024]{1,0:T(8,128)(2,1)}), bf16[1536,1024]{1,0:T(8,128)(2,1)}) %all-gather.22.cloned.1.call-update) | async-done | bytes 3145744 | tf_op jit(solution)/shard_map/all_gather | solution.py:136
  358.7 4.1 fusion.72
  362.7 34.8 %all-gather.24.cloned.1.call-done = bf16[1536,1024]{1,0:T(8,128)(2,1)} async-done(((bf16[192,1024]{1,0:T(8,128)(2,1)}), bf16[1536,1024]{1,0:T(8,128)(2,1)}) %all-gather.24.cloned.1.call-update) | async-done | bytes 3145744 | tf_op jit(solution)/shard_map/all_gather | solution.py:137
  397.5 3.9 fusion.66
  401.4 35.0 %all-gather.20.cloned.1.call-done = bf16[1536,1024]{1,0:T(8,128)(2,1)} async-done(((bf16[192,1024]{1,0:T(8,128)(2,1)}), bf16[1536,1024]{1,0:T(8,128)(2,1)}) %all-gather.20.cloned.1.call-update) | async-done | bytes 3145744 | tf_op jit(solution)/shard_map/all_gather | solution.py:135
  436.4 5.1 multiply_convert_fusion.2
  448.4 57.5 %all-reduce.16.cloned.1.call-done = f32[4,64,1536]{2,1,0:T(8,128)} async-done(((f32[4,64,1536]{2,1,0:T(8,128)}), f32[4,64,1536]{2,1,0:T(8,128)}) %all-reduce.16.cloned.1.call-update) | async-done | bytes 1572880 | tf_op jit(solution)/shard_map/psum | solution.py:320
  505.9 2.6 multiply_reduce_fusion
  513.3 95.8 %while.72 = (s32[]{:T(128)}, f32[4,3,64,128]{3,2,1,0:T(8,128)}, f32[4,3,64,128]{3,2,1,0:T(8,128)}, f32[4,3,128,128]{2,3,1,0:T(8,128)S(1)}, f32[4,3,64,128]{3,2,1...) while((s32[]{:T(128)}, f32[4,3,64,128]{3,2,1,0:T(8,128)}, ...), condition=%wide.region_18.19_spmd.clone, body=%wide.region_17.18_spmd.clone.sunk | while | flops 971800640 | bytes 25902632 | solution.py:374
  528.5 2.9 fusion.412
  531.4 3.5 convolution_add_fusion.23
  535.0 5.3 collective-permute-done.3
  561.3 3.2 fusion.412
  564.5 3.6 convolution_add_fusion.23
  568.1 5.0 collective-permute-done.3
  593.2 3.2 fusion.412
  596.4 3.6 convolution_add_fusion.23
  600.0 4.1 collective-permute-done.3
  611.1 2.6 fusion.173
  618.5 2.8 fusion.153
  644.7 2.9 fusion.83
  658.2 3.8 fusion.65
  663.1 3.7 bitcast_convert_fusion.2
  666.9 3.8 bitcast_convert_fusion.1
  671.8 4.2 fusion.87
  681.7 2.7 fusion.86
  687.4 12.0 %reduce-scatter.25.cloned.1.call-done = bf16[768,384]{1,0:T(8,128)(2,1)} async-done(((bf16[1536,384]{1,0:T(8,128)(2,1)}), bf16[768,384]{1,0:T(8,128)(2,1)}) %reduce-scatter.25.cloned.1.call-update) | async-done | bytes 589840 | tf_op jit(solution)/shard_map/reduce_scatter | solution.py:413
  699.5 14.1 %reduce-scatter.53.cloned.1.call-done = bf16[768,1024]{0,1:T(8,128)(2,1)} async-done(((bf16[1536,1024]{0,1:T(8,128)(2,1)}), bf16[768,1024]{0,1:T(8,128)(2,1)}) %reduce-scatter.53.cloned.1.call-update) | async-done | bytes 1572880 | tf_op jit(solution)/shard_map/reduce_scatter | solution.py:413
  713.6 2.6 copy.257
  716.3 11.6 %reduce-scatter.45.cloned.1.call-done = bf16[768,1024]{1,0:T(8,128)(2,1)} async-done(((bf16[1536,1024]{1,0:T(8,128)(2,1)}), bf16[768,1024]{1,0:T(8,128)(2,1)}) %reduce-scatter.45.cloned.1.call-update) | async-done | bytes 1572880 | tf_op jit(solution)/shard_map/reduce_scatter | solution.py:413
  728.0 14.2 %reduce-scatter.49.cloned.1.call-done = bf16[768,1024]{1,0:T(8,128)(2,1)} async-done(((bf16[1536,1024]{1,0:T(8,128)(2,1)}), bf16[768,1024]{1,0:T(8,128)(2,1)}) %reduce-scatter.49.cloned.1.call-update) | async-done | bytes 1572880 | tf_op jit(solution)/shard_map/reduce_scatter | solution.py:413
  744.7 20.2 %reduce-scatter.57.cloned.1.call-done = bf16[192,3]{1,0:T(8,128)(2,1)} async-done(((bf16[768,3]{1,0:T(8,128)(2,1)}), bf16[192,3]{1,0:T(8,128)(2,1)}) %reduce-scatter.57.cloned.1.call-update) | async-done | bytes 1168
  766.5 61.5 %all-reduce.18.cloned.1.call-done = (bf16[4,64,1536]{2,1,0:T(8,128)(2,1)}, bf16[4,64,1536]{2,1,0:T(8,128)(2,1)}) async-done(((bf16[4,64,1536]{2,1,0:T(8,128)(2,1)}, bf16[4,64,1536]{2,1,0:T(8,128)(2,1)}), (bf16[4,64,1536]{2,1,0:T(8,128)(2,1)}, bf16[4,64,1536]{2,1,0:T(8,128)(2,1)})) %all-reduce.18.cloned.1.call-update) | async-done | bytes 1572880 | tf_op jit(solution)/shard_map/psum | solution.py:308
  829.7 2.5 all-reduce.9
  832.4 12.1 %all-reduce.8 = (bf16[768]{0:T(1024)(128)(2,1)S(1)}, bf16[768]{0:T(1024)(128)(2,1)S(1)}) all-reduce(bf16[768]{0:T(1024)(128)(2,1)S(1)} %dynamic-slice.3, bf16[768]{0:T(1024)(128)(2,1)S(1)} %dynamic-slice.7), channel_id=3, replica_groups=mesh['fsdp'=2,'ctx'=4,'tp'=4] {'ctx'}, use_global_device_ids=true, to_apply=%region_25.26.clone | all-reduce | flops 1536 | bytes 6144
  848.4 3.8 reduce-scatter.43.cloned.1.call-done
  853.8 21.4 %reduce-scatter.39.cloned.1.call-done = bf16[192,384]{1,0:T(8,128)(2,1)} async-done(((bf16[768,384]{1,0:T(8,128)(2,1)}), bf16[192,384]{1,0:T(8,128)(2,1)}) %reduce-scatter.39.cloned.1.call-update) | async-done | bytes 147472 | tf_op jit(solution)/shard_map/reduce_scatter | solution.py:414
  876.9 21.0 %reduce-scatter.35.cloned.1.call-done = bf16[192,384]{1,0:T(8,128)(2,1)} async-done(((bf16[768,384]{1,0:T(8,128)(2,1)}), bf16[192,384]{1,0:T(8,128)(2,1)}) %reduce-scatter.35.cloned.1.call-update) | async-done | bytes 147472 | tf_op jit(solution)/shard_map/reduce_scatter | solution.py:414
  899.5 21.0 %reduce-scatter.31.cloned.1.call-done = bf16[192,384]{1,0:T(8,128)(2,1)} async-done(((bf16[768,384]{1,0:T(8,128)(2,1)}), bf16[192,384]{1,0:T(8,128)(2,1)}) %reduce-scatter.31.cloned.1.call-update) | async-done | bytes 147472 | tf_op jit(solution)/shard_map/reduce_scatter | solution.py:414
  922.2 21.0 %reduce-scatter.27.cloned.1.call-done = bf16[192,384]{1,0:T(8,128)(2,1)} async-done(((bf16[768,384]{1,0:T(8,128)(2,1)}), bf16[192,384]{1,0:T(8,128)(2,1)}) %reduce-scatter.27.cloned.1.call-update) | async-done | bytes 147472 | tf_op jit(solution)/shard_map/reduce_scatter | solution.py:414
  944.8 34.3 %reduce-scatter.59.cloned.1.call-done = bf16[192,1024]{1,0:T(8,128)(2,1)} async-done(((bf16[768,1024]{1,0:T(8,128)(2,1)}), bf16[192,1024]{1,0:T(8,128)(2,1)}) %reduce-scatter.59.cloned.1.call-update) | async-done | bytes 393232
  981.4 34.4 %reduce-scatter.47.cloned.1.call-done = bf16[192,1024]{1,0:T(8,128)(2,1)} async-done(((bf16[768,1024]{1,0:T(8,128)(2,1)}), bf16[192,1024]{1,0:T(8,128)(2,1)}) %reduce-scatter.47.cloned.1.call-update) | async-done | bytes 393232 | tf_op jit(solution)/shard_map/reduce_scatter | solution.py:414
  1017.8 34.8 %reduce-scatter.51.cloned.1.call-done = bf16[192,1024]{1,0:T(8,128)(2,1)} async-done(((bf16[768,1024]{1,0:T(8,128)(2,1)}), bf16[192,1024]{1,0:T(8,128)(2,1)}) %reduce-scatter.51.cloned.1.call-update) | async-done | bytes 393232 | tf_op jit(solution)/shard_map/reduce_scatter | solution.py:414
  (584 shorter events, 223.1 us)
Async XLA Ops:
  7.2 51.5 %copy-start.21 = (bf16[4,64,1536]{2,1,0:T(8,128)(2,1)S(1)}, bf16[4,64,1536]{2,1,0:T(8,128)(2,1)}, u32[]{:S(2)}) copy-start(bf16[4,64,1536]{2,1,0:T(8,128)(2,1)} %param.21) | copy-start | bytes 2359300
  7.2 54.9 %all-gather.14.cloned.1.call-start = ((), (), s32[]{:S(2)}) async-start(), calls=%async_computation.20 | async-start | bytes 1327104 | tf_op jit(solution)/shard_map/all_gather | solution.py:131
  7.9 51.9 %copy-start.117 = (s32[4,64]{1,0:T(4,128)S(1)}, s32[4,64]{1,0:T(4,128)}, u32[]{:S(2)}) copy-start(s32[4,64]{1,0:T(4,128)} %param.22) | copy-start | bytes 3076
  7.9 52.1 %copy-start.122 = (s32[4,1]{0,1:T(1,128)S(1)}, s32[4,1]{0,1:T(1,128)}, u32[]{:S(2)}) copy-start(s32[4,1]{0,1:T(1,128)} %param.23) | copy-start | bytes 52
  8.0 56.3 %all-gather.12.cloned.1.call-start = ((), (), s32[]{:S(2)}) async-start(), calls=%async_computation.19 | async-start | bytes 1327104 | tf_op jit(solution)/shard_map/all_gather | solution.py:129
  8.7 75.2 %all-gather.10.cloned.1.call-start = ((), (), s32[]{:S(2)}) async-start(), calls=%async_computation.18 | async-start | bytes 1327104 | tf_op jit(solution)/shard_map/all_gather | solution.py:128
  9.4 147.6 %all-gather.16.cloned.1.call-start = ((), (), s32[]{:S(2)}) async-start(), calls=%async_computation.21 | async-start | bytes 1327104 | tf_op jit(solution)/shard_map/all_gather | solution.py:130
  10.0 243.5 %all-gather.18.cloned.1.call-start = ((), (), s32[]{:S(2)}) async-start(), calls=%async_computation.22 | async-start | bytes 1327104 | tf_op jit(solution)/shard_map/all_gather | solution.py:133
  10.6 308.1 %all-reduce.14.cloned.1.call-start = ((), (), s32[]{:S(2)}) async-start(), calls=%async_computation.23 | async-start | bytes 3145728 | tf_op jit(solution)/shard_map/psum | solution.py:299
  10.7 79.0 %copy-start.90 = (pred[64,64]{1,0:T(8,128)(4,1)}, pred[64,64]{1,0:T(8,128)(4,1)S(1)}, u32[]{:S(2)}) copy-start(pred[64,64]{1,0:T(8,128)(4,1)S(1)} %iota_compare_fusion.2) | copy-start | bytes 12292
  10.7 79.0 %copy-start.92 = (pred[64,64]{1,0:T(8,128)(4,1)}, pred[64,64]{1,0:T(8,128)(4,1)S(1)}, u32[]{:S(2)}) copy-start(pred[64,64]{1,0:T(8,128)(4,1)S(1)} %iota_compare_fusion.3) | copy-start | bytes 12292
  10.7 79.0 %copy-start.106 = (pred[64,64]{1,0:T(8,128)(4,1)}, pred[64,64]{1,0:T(8,128)(4,1)S(1)}, u32[]{:S(2)}) copy-start(pred[64,64]{1,0:T(8,128)(4,1)S(1)} %iota_compare_fusion.1) | copy-start | bytes 12292
  35.3 121.7 %copy-start.94 = (f32[1536]{0:T(1024)}, f32[1536]{0:T(1024)S(1)}, u32[]{:S(2)}) copy-start(f32[1536]{0:T(1024)S(1)} %convert_element_type.291) | copy-start | bytes 18436
  85.8 70.6 %copy-start.26 = (f32[4,8,3,8,128]{4,3,2,1,0:T(8,128)}, f32[4,8,3,8,128]{4,3,2,1,0:T(8,128)S(1)}, u32[]{:S(2)}) copy-start(f32[4,8,3,8,128]{4,3,2,1,0:T(8,128)S(1)} %convolution_bitcast_fusion.9) | copy-start | bytes 1179652
  89.7 64.5 %copy-start.28 = (f32[4,3,64,64]{3,2,1,0:T(8,128)}, f32[4,3,64,64]{3,2,1,0:T(8,128)S(1)}, u32[]{:S(2)}) copy-start(f32[4,3,64,64]{3,2,1,0:T(8,128)S(1)} %convolution_select_fusion.1) | copy-start | bytes 589828
  89.7 63.9 %copy-start.45 = (f32[4,3,64,64]{3,2,1,0:T(8,128)S(1)}, f32[4,3,64,64]{3,2,1,0:T(8,128)}, u32[]{:S(2)}) copy-start(f32[4,3,64,64]{3,2,1,0:T(8,128)} %convolution_select_fusion.3) | copy-start | bytes 589828
  159.1 84.4 %copy-start.40 = (bf16[4,3,64,128]{3,2,1,0:T(8,128)(2,1)}, bf16[4,3,64,128]{3,2,1,0:T(8,128)(2,1)S(1)}, u32[]{:S(2)}) copy-start(bf16[4,3,64,128]{3,2,1,0:T(8,128)(2,1)S(1)} %copy.186) | copy-start | bytes 589828
  161.6 81.9 %copy-start.16 = (f32[4,3,64,64]{2,3,1,0:T(8,128)}, f32[4,3,64,64]{2,3,1,0:T(8,128)S(1)}, u32[]{:S(2)}) copy-start(f32[4,3,64,64]{2,3,1,0:T(8,128)S(1)} %get-tuple-element.1238) | copy-start | bytes 589828
  164.7 22.3 %collective-permute-start.2 = (bf16[4,3,128,128]{3,2,1,0:T(8,128)(2,1)}, bf16[4,3,128,128]{3,2,1,0:T(8,128)(2,1)S(1)}, u32[]{:S(2)}, u32[]{:S(2)}) collective-permute-start(bf16[4,3,128,128]{3,2,1,0:T(8,128)(2,1)} %get-tuple-element.1515), channel_id=1, source_target_pairs={{0,4},{4,8},{8,12},{1,5},{5,9},{9,13},{2,6},{6,10},{10,14},{3,7},{... | collective-permute-start | bytes 1179656 | tf_op jit(solution)/shard_map/while/body/eval_jaxpr/ppermute | solution.py:16
  168.1 13.9 %collective-permute-start = (bf16[4,3,64,128]{3,2,1,0:T(8,128)(2,1)}, bf16[4,3,64,128]{3,2,1,0:T(8,128)(2,1)S(1)}, u32[]{:S(2)}, u32[]{:S(2)}) collective-permute-start(bf16[4,3,64,128]{3,2,1,0:T(8,128)(2,1)} %get-tuple-element.1513), channel_id=1, source_target_pairs={{0,4},{4,8},{8,12},{1,5},{5,9},{9,13},{2,6},{6,10},{10,14},{3,7},{... | collective-permute-start | bytes 589832 | tf_op jit(solution)/shard_map/while/body/eval_jaxpr/ppermute | solution.py:16
  171.2 14.4 %collective-permute-start.1 = (bf16[4,3,64,128]{3,2,1,0:T(8,128)(2,1)}, bf16[4,3,64,128]{3,2,1,0:T(8,128)(2,1)S(1)}, u32[]{:S(2)}, u32[]{:S(2)}) collective-permute-start(bf16[4,3,64,128]{3,2,1,0:T(8,128)(2,1)} %get-tuple-element.1514), channel_id=1, source_target_pairs={{0,4},{4,8},{8,12},{1,5},{5,9},{9,13},{2,6},{6,10},{10,14},{3,7},{... | collective-permute-start | bytes 589832 | tf_op jit(solution)/shard_map/while/body/eval_jaxpr/ppermute | solution.py:16
  190.8 22.4 %collective-permute-start.2 = (bf16[4,3,128,128]{3,2,1,0:T(8,128)(2,1)}, bf16[4,3,128,128]{3,2,1,0:T(8,128)(2,1)S(1)}, u32[]{:S(2)}, u32[]{:S(2)}) collective-permute-start(bf16[4,3,128,128]{3,2,1,0:T(8,128)(2,1)} %get-tuple-element.1515), channel_id=1, source_target_pairs={{0,4},{4,8},{8,12},{1,5},{5,9},{9,13},{2,6},{6,10},{10,14},{3,7},{... | collective-permute-start | bytes 1179656 | tf_op jit(solution)/shard_map/while/body/eval_jaxpr/ppermute | solution.py:16
  195.1 14.1 %collective-permute-start = (bf16[4,3,64,128]{3,2,1,0:T(8,128)(2,1)}, bf16[4,3,64,128]{3,2,1,0:T(8,128)(2,1)S(1)}, u32[]{:S(2)}, u32[]{:S(2)}) collective-permute-start(bf16[4,3,64,128]{3,2,1,0:T(8,128)(2,1)} %get-tuple-element.1513), channel_id=1, source_target_pairs={{0,4},{4,8},{8,12},{1,5},{5,9},{9,13},{2,6},{6,10},{10,14},{3,7},{... | collective-permute-start | bytes 589832 | tf_op jit(solution)/shard_map/while/body/eval_jaxpr/ppermute | solution.py:16
  198.1 13.6 %collective-permute-start.1 = (bf16[4,3,64,128]{3,2,1,0:T(8,128)(2,1)}, bf16[4,3,64,128]{3,2,1,0:T(8,128)(2,1)S(1)}, u32[]{:S(2)}, u32[]{:S(2)}) collective-permute-start(bf16[4,3,64,128]{3,2,1,0:T(8,128)(2,1)} %get-tuple-element.1514), channel_id=1, source_target_pairs={{0,4},{4,8},{8,12},{1,5},{5,9},{9,13},{2,6},{6,10},{10,14},{3,7},{... | collective-permute-start | bytes 589832 | tf_op jit(solution)/shard_map/while/body/eval_jaxpr/ppermute | solution.py:16
  216.9 21.5 %collective-permute-start.2 = (bf16[4,3,128,128]{3,2,1,0:T(8,128)(2,1)}, bf16[4,3,128,128]{3,2,1,0:T(8,128)(2,1)S(1)}, u32[]{:S(2)}, u32[]{:S(2)}) collective-permute-start(bf16[4,3,128,128]{3,2,1,0:T(8,128)(2,1)} %get-tuple-element.1515), channel_id=1, source_target_pairs={{0,4},{4,8},{8,12},{1,5},{5,9},{9,13},{2,6},{6,10},{10,14},{3,7},{... | collective-permute-start | bytes 1179656 | tf_op jit(solution)/shard_map/while/body/eval_jaxpr/ppermute | solution.py:16
  221.2 13.7 %collective-permute-start = (bf16[4,3,64,128]{3,2,1,0:T(8,128)(2,1)}, bf16[4,3,64,128]{3,2,1,0:T(8,128)(2,1)S(1)}, u32[]{:S(2)}, u32[]{:S(2)}) collective-permute-start(bf16[4,3,64,128]{3,2,1,0:T(8,128)(2,1)} %get-tuple-element.1513), channel_id=1, source_target_pairs={{0,4},{4,8},{8,12},{1,5},{5,9},{9,13},{2,6},{6,10},{10,14},{3,7},{... | collective-permute-start | bytes 589832 | tf_op jit(solution)/shard_map/while/body/eval_jaxpr/ppermute | solution.py:16
  224.3 12.7 %collective-permute-start.1 = (bf16[4,3,64,128]{3,2,1,0:T(8,128)(2,1)}, bf16[4,3,64,128]{3,2,1,0:T(8,128)(2,1)S(1)}, u32[]{:S(2)}, u32[]{:S(2)}) collective-permute-start(bf16[4,3,64,128]{3,2,1,0:T(8,128)(2,1)} %get-tuple-element.1514), channel_id=1, source_target_pairs={{0,4},{4,8},{8,12},{1,5},{5,9},{9,13},{2,6},{6,10},{10,14},{3,7},{... | collective-permute-start | bytes 589832 | tf_op jit(solution)/shard_map/while/body/eval_jaxpr/ppermute | solution.py:16
  253.5 257.7 %copy-start.7 = (f32[4,3,64,128]{3,2,1,0:T(8,128)}, f32[4,3,64,128]{3,2,1,0:T(8,128)S(1)}, u32[]{:S(2)}) copy-start(f32[4,3,64,128]{3,2,1,0:T(8,128)S(1)} %get-tuple-element.859) | copy-start | bytes 1179652
  257.0 61.7 %copy-start.22 = (bf16[4,64,1536]{2,1,0:T(8,128)(2,1)S(1)}, bf16[4,64,1536]{2,1,0:T(8,128)(2,1)}, u32[]{:S(2)}) copy-start(bf16[4,64,1536]{2,1,0:T(8,128)(2,1)} %param.21) | copy-start | bytes 2359300
  257.0 101.7 %all-gather.22.cloned.1.call-start = ((), (), s32[]{:S(2)}) async-start(), calls=%async_computation.25 | async-start | bytes 3538944 | tf_op jit(solution)/shard_map/all_gather | solution.py:136
  257.8 139.8 %all-gather.24.cloned.1.call-start = ((), (), s32[]{:S(2)}) async-start(), calls=%async_computation.26 | async-start | bytes 3538944 | tf_op jit(solution)/shard_map/all_gather | solution.py:137
  258.5 177.9 %all-gather.20.cloned.1.call-start = ((), (), s32[]{:S(2)}) async-start(), calls=%async_computation.24 | async-start | bytes 3538944 | tf_op jit(solution)/shard_map/all_gather | solution.py:135
  259.2 246.6 %all-reduce.16.cloned.1.call-start = ((), (), s32[]{:S(2)}) async-start(), calls=%async_computation.27 | async-start | bytes 3145728 | tf_op jit(solution)/shard_map/psum | solution.py:320
  322.0 75.5 %copy-start.78 = (bf16[4,64,1536]{2,1,0:T(8,128)(2,1)S(1)}, bf16[4,64,1536]{2,1,0:T(8,128)(2,1)}, u32[]{:S(2)}) copy-start(bf16[4,64,1536]{2,1,0:T(8,128)(2,1)} %param.35) | copy-start | bytes 2359300
  446.0 235.6 %reduce-scatter.55.cloned.1.call-start = ((), (), s32[]{:S(2)}) async-start(), calls=%async_computation.43 | async-start | bytes 589824
  521.8 23.2 %collective-permute-start.5 = (bf16[4,3,128,128]{2,3,1,0:T(8,128)(2,1)}, bf16[4,3,128,128]{2,3,1,0:T(8,128)(2,1)}, u32[]{:S(2)}, u32[]{:S(2)}) collective-permute-start(bf16[4,3,128,128]{2,3,1,0:T(8,128)(2,1)} %fusion.411), channel_id=1, source_target_pairs={{4,0},{8,4},{12,8},{5,1},{9,5},{13,9},{6,2},{10,6},{14,10},{7,3},{... | collective-permute-start | bytes 1179656 | tf_op jit(solution)/shard_map/while/body/eval_jaxpr/ppermute | solution.py:16
  525.0 15.2 %collective-permute-start.3 = (bf16[4,3,64,128]{3,2,1,0:T(8,128)(2,1)}, bf16[4,3,64,128]{3,2,1,0:T(8,128)(2,1)}, u32[]{:S(2)}, u32[]{:S(2)}) collective-permute-start(bf16[4,3,64,128]{3,2,1,0:T(8,128)(2,1)} %fusion.408), channel_id=1, source_target_pairs={{4,0},{8,4},{12,8},{5,1},{9,5},{13,9},{6,2},{10,6},{14,10},{7,3},{... | collective-permute-start | bytes 589832 | tf_op jit(solution)/shard_map/while/body/eval_jaxpr/ppermute | solution.py:16
  527.2 16.1 %collective-permute-start.4 = (bf16[4,3,64,128]{3,2,1,0:T(8,128)(2,1)}, bf16[4,3,64,128]{3,2,1,0:T(8,128)(2,1)}, u32[]{:S(2)}, u32[]{:S(2)}) collective-permute-start(bf16[4,3,64,128]{3,2,1,0:T(8,128)(2,1)} %fusion.409), channel_id=1, source_target_pairs={{4,0},{8,4},{12,8},{5,1},{9,5},{13,9},{6,2},{10,6},{14,10},{7,3},{... | collective-permute-start | bytes 589832 | tf_op jit(solution)/shard_map/while/body/eval_jaxpr/ppermute | solution.py:16
  554.6 22.3 %collective-permute-start.5 = (bf16[4,3,128,128]{2,3,1,0:T(8,128)(2,1)}, bf16[4,3,128,128]{2,3,1,0:T(8,128)(2,1)}, u32[]{:S(2)}, u32[]{:S(2)}) collective-permute-start(bf16[4,3,128,128]{2,3,1,0:T(8,128)(2,1)} %fusion.411), channel_id=1, source_target_pairs={{4,0},{8,4},{12,8},{5,1},{9,5},{13,9},{6,2},{10,6},{14,10},{7,3},{... | collective-permute-start | bytes 1179656 | tf_op jit(solution)/shard_map/while/body/eval_jaxpr/ppermute | solution.py:16
  557.8 15.3 %collective-permute-start.3 = (bf16[4,3,64,128]{3,2,1,0:T(8,128)(2,1)}, bf16[4,3,64,128]{3,2,1,0:T(8,128)(2,1)}, u32[]{:S(2)}, u32[]{:S(2)}) collective-permute-start(bf16[4,3,64,128]{3,2,1,0:T(8,128)(2,1)} %fusion.408), channel_id=1, source_target_pairs={{4,0},{8,4},{12,8},{5,1},{9,5},{13,9},{6,2},{10,6},{14,10},{7,3},{... | collective-permute-start | bytes 589832 | tf_op jit(solution)/shard_map/while/body/eval_jaxpr/ppermute | solution.py:16
  560.0 15.2 %collective-permute-start.4 = (bf16[4,3,64,128]{3,2,1,0:T(8,128)(2,1)}, bf16[4,3,64,128]{3,2,1,0:T(8,128)(2,1)}, u32[]{:S(2)}, u32[]{:S(2)}) collective-permute-start(bf16[4,3,64,128]{3,2,1,0:T(8,128)(2,1)} %fusion.409), channel_id=1, source_target_pairs={{4,0},{8,4},{12,8},{5,1},{9,5},{13,9},{6,2},{10,6},{14,10},{7,3},{... | collective-permute-start | bytes 589832 | tf_op jit(solution)/shard_map/while/body/eval_jaxpr/ppermute | solution.py:16
  586.5 21.4 %collective-permute-start.5 = (bf16[4,3,128,128]{2,3,1,0:T(8,128)(2,1)}, bf16[4,3,128,128]{2,3,1,0:T(8,128)(2,1)}, u32[]{:S(2)}, u32[]{:S(2)}) collective-permute-start(bf16[4,3,128,128]{2,3,1,0:T(8,128)(2,1)} %fusion.411), channel_id=1, source_target_pairs={{4,0},{8,4},{12,8},{5,1},{9,5},{13,9},{6,2},{10,6},{14,10},{7,3},{... | collective-permute-start | bytes 1179656 | tf_op jit(solution)/shard_map/while/body/eval_jaxpr/ppermute | solution.py:16
  589.7 14.4 %collective-permute-start.3 = (bf16[4,3,64,128]{3,2,1,0:T(8,128)(2,1)}, bf16[4,3,64,128]{3,2,1,0:T(8,128)(2,1)}, u32[]{:S(2)}, u32[]{:S(2)}) collective-permute-start(bf16[4,3,64,128]{3,2,1,0:T(8,128)(2,1)} %fusion.408), channel_id=1, source_target_pairs={{4,0},{8,4},{12,8},{5,1},{9,5},{13,9},{6,2},{10,6},{14,10},{7,3},{... | collective-permute-start | bytes 589832 | tf_op jit(solution)/shard_map/while/body/eval_jaxpr/ppermute | solution.py:16
  591.9 14.3 %collective-permute-start.4 = (bf16[4,3,64,128]{3,2,1,0:T(8,128)(2,1)}, bf16[4,3,64,128]{3,2,1,0:T(8,128)(2,1)}, u32[]{:S(2)}, u32[]{:S(2)}) collective-permute-start(bf16[4,3,64,128]{3,2,1,0:T(8,128)(2,1)} %fusion.409), channel_id=1, source_target_pairs={{4,0},{8,4},{12,8},{5,1},{9,5},{13,9},{6,2},{10,6},{14,10},{7,3},{... | collective-permute-start | bytes 589832 | tf_op jit(solution)/shard_map/while/body/eval_jaxpr/ppermute | solution.py:16
  631.5 53.0 %reduce-scatter.41.cloned.1.call-start = ((), (), s32[]{:S(2)}) async-start(), calls=%async_computation.36 | async-start | bytes 1769472 | tf_op jit(solution)/shard_map/reduce_scatter | solution.py:413
  633.2 52.1 %reduce-scatter.37.cloned.1.call-start = ((), (), s32[]{:S(2)}) async-start(), calls=%async_computation.34 | async-start | bytes 1769472 | tf_op jit(solution)/shard_map/reduce_scatter | solution.py:413
  643.7 42.3 %reduce-scatter.33.cloned.1.call-start = ((), (), s32[]{:S(2)}) async-start(), calls=%async_computation.32 | async-start | bytes 1769472 | tf_op jit(solution)/shard_map/reduce_scatter | solution.py:413
  647.7 39.6 %reduce-scatter.29.cloned.1.call-start = ((), (), s32[]{:S(2)}) async-start(), calls=%async_computation.30 | async-start | bytes 1769472 | tf_op jit(solution)/shard_map/reduce_scatter | solution.py:413
  653.1 46.3 %reduce-scatter.25.cloned.1.call-start = ((), (), s32[]{:S(2)}) async-start(), calls=%async_computation.28 | async-start | bytes 1769472 | tf_op jit(solution)/shard_map/reduce_scatter | solution.py:413
  658.1 55.5 %reduce-scatter.53.cloned.1.call-start = ((), (), s32[]{:S(2)}) async-start(), calls=%async_computation.42 | async-start | bytes 4718592 | tf_op jit(solution)/shard_map/reduce_scatter | solution.py:413
  662.0 65.9 %reduce-scatter.45.cloned.1.call-start = ((), (), s32[]{:S(2)}) async-start(), calls=%async_computation.38 | async-start | bytes 4718592 | tf_op jit(solution)/shard_map/reduce_scatter | solution.py:413
  666.9 75.3 %reduce-scatter.49.cloned.1.call-start = ((), (), s32[]{:S(2)}) async-start(), calls=%async_computation.40 | async-start | bytes 4718592 | tf_op jit(solution)/shard_map/reduce_scatter | solution.py:413
  670.8 94.2 %reduce-scatter.57.cloned.1.call-start = ((), (), s32[]{:S(2)}) async-start(), calls=%async_computation.44 | async-start | bytes 245760
  681.6 146.3 %all-reduce.18.cloned.1.call-start = ((), (), s32[]{:S(2)}) async-start(), calls=%async_computation.46 | async-start | bytes 3145728 | tf_op jit(solution)/shard_map/psum | solution.py:308
  684.4 167.8 %reduce-scatter.43.cloned.1.call-start = ((), (), s32[]{:S(2)}) async-start(), calls=%async_computation.37 | async-start | bytes 737280 | tf_op jit(solution)/shard_map/reduce_scatter | solution.py:414
  685.2 190.0 %reduce-scatter.39.cloned.1.call-start = ((), (), s32[]{:S(2)}) async-start(), calls=%async_computation.35 | async-start | bytes 737280 | tf_op jit(solution)/shard_map/reduce_scatter | solution.py:414
  685.9 211.9 %reduce-scatter.35.cloned.1.call-start = ((), (), s32[]{:S(2)}) async-start(), calls=%async_computation.33 | async-start | bytes 737280 | tf_op jit(solution)/shard_map/reduce_scatter | solution.py:414
  686.5 234.0 %reduce-scatter.31.cloned.1.call-start = ((), (), s32[]{:S(2)}) async-start(), calls=%async_computation.31 | async-start | bytes 737280 | tf_op jit(solution)/shard_map/reduce_scatter | solution.py:414
  687.4 255.8 %reduce-scatter.27.cloned.1.call-start = ((), (), s32[]{:S(2)}) async-start(), calls=%async_computation.29 | async-start | bytes 737280 | tf_op jit(solution)/shard_map/reduce_scatter | solution.py:414
  699.4 279.7 %reduce-scatter.59.cloned.1.call-start = ((), (), s32[]{:S(2)}) async-start(), calls=%async_computation.45 | async-start | bytes 1966080
  716.2 299.6 %reduce-scatter.47.cloned.1.call-start = ((), (), s32[]{:S(2)}) async-start(), calls=%async_computation.39 | async-start | bytes 1966080 | tf_op jit(solution)/shard_map/reduce_scatter | solution.py:414
  727.9 100.0 %copy-start.116 = (f32[4,64]{1,0:T(4,128)S(1)}, f32[4,64]{1,0:T(4,128)}, u32[]{:S(2)}) copy-start(f32[4,64]{1,0:T(4,128)} %copy-done.110) | copy-start | bytes 3076
  727.9 324.6 %reduce-scatter.51.cloned.1.call-start = ((), (), s32[]{:S(2)}) async-start(), calls=%async_computation.41 | async-start | bytes 1966080 | tf_op jit(solution)/shard_map/reduce_scatter | solution.py:414
  742.2 87.5 %copy-start.118 = (bf16[1536]{0:T(1024)(128)(2,1)S(1)}, bf16[1536]{0:T(1024)(128)(2,1)}, u32[]{:S(2)}) copy-start(bf16[1536]{0:T(1024)(128)(2,1)} %get-tuple-element.1134) | copy-start | bytes 9220
  (121 other events, 491.0 us)
Sparse Core Ops, SparseCore 0:
  9.6 26.2 all-gather.13
  37.5 22.5 all-gather.11
  61.7 22.1 all-gather.9
  85.3 22.8 all-gather.15
  109.7 22.3 all-gather.17
  257.1 61.4 all-reduce.13
  320.3 38.2 all-gather.21
  360.3 37.1 all-gather.23
  399.2 37.1 all-gather.19
  446.1 59.7 all-reduce.15
  631.6 7.4 reduce-scatter.54
  641.3 9.7 reduce-scatter.40
  653.4 9.8 reduce-scatter.36
  665.5 9.8 reduce-scatter.32
  677.5 9.8 reduce-scatter.28
  689.5 9.8 reduce-scatter.24
  701.5 12.0 reduce-scatter.52
  715.8 12.0 reduce-scatter.44
  730.1 12.0 reduce-scatter.48
  744.4 20.5 reduce-scatter.56
  768.6 59.2 all-reduce.17
  830.3 21.8 reduce-scatter.42
  854.6 20.5 reduce-scatter.38
  877.5 20.3 reduce-scatter.34
  900.2 20.2 reduce-scatter.30
  922.8 20.3 reduce-scatter.26
  945.4 33.6 reduce-scatter.58
  981.5 34.2 reduce-scatter.46
  1018.2 34.2 reduce-scatter.50
